TPU v7x, 512 devices: a whole 4x8x8 slice. The times are simulated.
512 devices in a mesh: bx: 16 (over x, z_hi), by: 4 (over z_lo, core), bz: 8 (over y).
Axes of the slice: x: 4, y: 8, z: 8 (z_hi: 4, z_lo: 2; z = z_hi * 2 + z_lo), core: 2. Of those that a mesh axis runs over, the one named last changes fastest.
Arguments:
- forcing: float32 [256, 256, 512], P('bx', 'bz', 'by'), may hold values from -6 to 6
- start: float32 [256, 256, 512], P('bx', 'bz', 'by'), may hold values from -2 to 2
- element_class_index: int32 [64, 64, 128], P('bx', 'bz', 'by'), may hold values from 0 to 15
- class_coef: float32 [3, 16], replicated, may hold values from 0.3 to 3
Outputs:
- solution: float32 [256, 256, 512], P('bx', 'bz', 'by')
- residual: float32 [256, 256, 512], P('bx', 'bz', 'by')
All inputs are finite; a program needn't handle non-finite values.
Results may differ from a plain program's by a relative error of at most 0.015.
Values may be sent and summed in bfloat16 or wider, within the bound.
A program may use at most 64 MiB of HBM per device.

v0:
```python
import math
import jax
import jax.numpy as jnp
from jax import lax
from jax.sharding import PartitionSpec as P

CYCLES = 2
FACE_PENALTY = 2.0
DAMPING = 0.6666666666666666


def extended(value, sides, width):
    for axis, dim in sides:
        devices, length = (lax.axis_size(axis), value.shape[dim])
        up = [(i, (i + 1) % devices) for i in range(devices - 1)]
        down = [(j, i) for i, j in up]
        last = lax.slice_in_dim(value, length - width, length, axis=dim)
        first = lax.slice_in_dim(value, 0, width, axis=dim)
        before = lax.ppermute(last, axis, up)
        after = lax.ppermute(first, axis, down)
        value = jnp.concatenate([before, value, after], axis=dim)
    return value


def face_factor(count):
    edges = jnp.arange(count + 1, dtype=jnp.int32)
    return jnp.where(edges % 4 == 0, FACE_PENALTY, 1.0).astype(jnp.float32)


def edge_weights(kappa_pad):
    inner_x = kappa_pad[:, 1:-1, 1:-1]
    weight_x = face_factor(inner_x.shape[0] - 2)[:, None, None] * (
        (inner_x[:-1] + inner_x[1:]) * 0.5
    )
    inner_z = kappa_pad[1:-1, :, 1:-1]
    weight_z = face_factor(inner_z.shape[1] - 2)[None, :, None] * (
        (inner_z[:, :-1] + inner_z[:, 1:]) * 0.5
    )
    inner_y = kappa_pad[1:-1, 1:-1, :]
    quadrature_weight_y = face_factor(inner_y.shape[2] - 2)[None, None, :] * (
        (inner_y[:, :, :-1] + inner_y[:, :, 1:]) * 0.5
    )
    return (weight_x, weight_z, quadrature_weight_y)


def operator_diagonal(weights, sigma_node):
    weight_x, weight_z, quadrature_weight_y = weights
    total = sigma_node + (weight_x[:-1] + weight_x[1:])
    total = total + (weight_z[:, :-1] + weight_z[:, 1:])
    return total + (quadrature_weight_y[:, :, :-1] + quadrature_weight_y[:, :, 1:])


def apply_operator(field_pad, weights, sigma_node):
    weight_x, weight_z, quadrature_weight_y = weights
    centre = field_pad[1:-1, 1:-1, 1:-1]
    total = sigma_node * centre
    total = (
        total
        + weight_x[:-1] * (centre - field_pad[:-2, 1:-1, 1:-1])
        + weight_x[1:] * (centre - field_pad[2:, 1:-1, 1:-1])
    )
    total = (
        total
        + weight_z[:, :-1] * (centre - field_pad[1:-1, :-2, 1:-1])
        + weight_z[:, 1:] * (centre - field_pad[1:-1, 2:, 1:-1])
    )
    total = (
        total
        + quadrature_weight_y[:, :, :-1] * (centre - field_pad[1:-1, 1:-1, :-2])
        + quadrature_weight_y[:, :, 1:] * (centre - field_pad[1:-1, 1:-1, 2:])
    )
    return total


def padded_field(field):
    return extended(field, (("bx", 0), ("bz", 1), ("by", 2)), 1)


def node_field(element_values):
    return jnp.repeat(jnp.repeat(jnp.repeat(element_values, 4, 0), 4, 1), 4, 2)


def restrict_matrix():
    return (
        jnp.array(
            [[1.0, 2.0 / 3.0, 1.0 / 3.0, 0.0], [0.0, 1.0 / 3.0, 2.0 / 3.0, 1.0]], dtype=jnp.float32
        )
        * 0.5
    )


def prolong_matrix():
    return jnp.array(
        [[1.0, 0.0], [2.0 / 3.0, 1.0 / 3.0], [1.0 / 3.0, 2.0 / 3.0], [0.0, 1.0]], dtype=jnp.float32
    )


def restrict_field(field):
    count_x, count_z, count_y = (field.shape[0] // 4, field.shape[1] // 4, field.shape[2] // 4)
    blocks = field.reshape(count_x, 4, count_z, 4, count_y, 4)
    matrix = restrict_matrix()
    blocks = jnp.einsum("ai,pizjyk->pazjyk", matrix, blocks, precision=lax.Precision.HIGHEST)
    blocks = jnp.einsum("bj,pazjyk->pazbyk", matrix, blocks, precision=lax.Precision.HIGHEST)
    blocks = jnp.einsum("ck,pazbyk->pazbyc", matrix, blocks, precision=lax.Precision.HIGHEST)
    return blocks.reshape(2 * count_x, 2 * count_z, 2 * count_y)


def prolong_field(coarse):
    count_x, count_z, count_y = (coarse.shape[0] // 2, coarse.shape[1] // 2, coarse.shape[2] // 2)
    blocks = coarse.astype(jnp.float32).reshape(count_x, 2, count_z, 2, count_y, 2)
    matrix = prolong_matrix()
    blocks = jnp.einsum("ia,pazbyc->pizbyc", matrix, blocks, precision=lax.Precision.HIGHEST)
    blocks = jnp.einsum("jb,pizbyc->pizjyc", matrix, blocks, precision=lax.Precision.HIGHEST)
    blocks = jnp.einsum("kc,pizjyc->pizjyk", matrix, blocks, precision=lax.Precision.HIGHEST)
    return blocks.reshape(4 * count_x, 4 * count_z, 4 * count_y)


def sine_rows(index_zero, count):
    index_one = index_zero + 1
    product = (index_one[:, None] * index_one[None, :]).astype(jnp.float32)
    return (jnp.sin(product * (math.pi / (count + 1))) * math.sqrt(2.0 / (count + 1))).astype(
        jnp.bfloat16
    )


def spectrum_values(index_zero, count):
    return 2.0 - 2.0 * jnp.cos((index_zero + 1).astype(jnp.float32) * (math.pi / (count + 1)))


def class_values(element_class_index, class_coef):
    labels = jnp.arange(class_coef.shape[1], dtype=jnp.int32)
    onehot = (element_class_index[..., None] == labels).astype(jnp.float32)
    return tuple((jnp.sum(onehot * class_coef[row], axis=-1) for row in range(3)))


def coarse_correction(resid, kappa_mean, sigma_mean):
    count_bx, count_by, count_bz = (lax.axis_size("bx"), lax.axis_size("by"), lax.axis_size("bz"))
    coarse = restrict_field(resid).astype(jnp.bfloat16)
    pencil = lax.all_to_all(coarse, "by", split_axis=0, concat_axis=2, tiled=True)
    count_y = pencil.shape[2]
    table_y = sine_rows(jnp.arange(count_y, dtype=jnp.int32), count_y)
    pencil = jnp.dot(pencil, table_y, preferred_element_type=jnp.float32).astype(jnp.bfloat16)
    pencil = lax.all_to_all(pencil, "bz", split_axis=2, concat_axis=1, tiled=True)
    count_z = pencil.shape[1]
    table_z = sine_rows(jnp.arange(count_z, dtype=jnp.int32), count_z)
    pencil = jnp.einsum("ab,xbc->xac", table_z, pencil, preferred_element_type=jnp.float32).astype(
        jnp.bfloat16
    )
    pencil = lax.all_to_all(pencil, ("bx", "by"), split_axis=1, concat_axis=0, tiled=True)
    count_x = pencil.shape[0]
    x_index = jnp.arange(count_x, dtype=jnp.int32)
    table_x = sine_rows(x_index, count_x)
    local_z = pencil.shape[1]
    local_y = pencil.shape[2]
    z_index = (lax.axis_index("bx") * count_by + lax.axis_index("by")) * local_z + jnp.arange(
        local_z, dtype=jnp.int32
    )
    y_index = lax.axis_index("bz") * local_y + jnp.arange(local_y, dtype=jnp.int32)
    eigen_x = spectrum_values(x_index, count_x)
    eigen_z = spectrum_values(z_index, local_z * count_bx * count_by)
    eigen_y = spectrum_values(y_index, local_y * count_bz)
    eigen_sum = (
        kappa_mean * (eigen_x[:, None, None] + eigen_z[None, :, None] + eigen_y[None, None, :])
        + sigma_mean
    )
    pencil = (
        jnp.einsum("ab,bzy->azy", table_x, pencil, preferred_element_type=jnp.float32) / eigen_sum
    ).astype(jnp.bfloat16)
    pencil = jnp.einsum("ab,bzy->azy", table_x, pencil, preferred_element_type=jnp.float32).astype(
        jnp.bfloat16
    )
    pencil = lax.all_to_all(pencil, ("bx", "by"), split_axis=0, concat_axis=1, tiled=True)
    pencil = jnp.einsum("ab,xbc->xac", table_z, pencil, preferred_element_type=jnp.float32).astype(
        jnp.bfloat16
    )
    pencil = lax.all_to_all(pencil, "bz", split_axis=1, concat_axis=2, tiled=True)
    pencil = jnp.dot(pencil, table_y, preferred_element_type=jnp.float32).astype(jnp.bfloat16)
    coarse = lax.all_to_all(pencil, "by", split_axis=2, concat_axis=0, tiled=True)
    return prolong_field(coarse)


def body(forcing, start, element_class_index, class_coef):
    kappa_elem, sigma_elem, beta_elem = class_values(element_class_index, class_coef)
    kappa_node = node_field(kappa_elem)
    sigma_node = node_field(sigma_elem)
    beta_node = node_field(beta_elem)
    kappa_pad = extended(kappa_node, (("bx", 0), ("bz", 1), ("by", 2)), 1)
    weights = edge_weights(kappa_pad)
    diagonal = operator_diagonal(weights, sigma_node)
    kappa_mean = jnp.mean(class_coef[0])
    sigma_mean = jnp.mean(class_coef[1])

    def nonlinear_residual(solution):
        return (
            forcing
            - apply_operator(padded_field(solution), weights, sigma_node)
            - beta_node * solution * solution * solution
        )

    solution = start
    for iteration in range(CYCLES):
        resid = nonlinear_residual(solution)
        smooth_one = DAMPING * resid / diagonal
        smooth_two = (
            smooth_one
            + DAMPING
            * (resid - apply_operator(padded_field(smooth_one), weights, sigma_node))
            / diagonal
        )
        solution = solution + smooth_two + coarse_correction(resid, kappa_mean, sigma_mean)
    return (solution, nonlinear_residual(solution))


def solution(mesh):
    in_specs = (P("bx", "bz", "by"), P("bx", "bz", "by"), P("bx", "bz", "by"), P())
    out_specs = (P("bx", "bz", "by"), P("bx", "bz", "by"))
    return jax.shard_map(body, mesh=mesh, in_specs=in_specs, out_specs=out_specs, check_vma=False)
```

profile of v0, /device:TPU:11, one launch (start us, length us, event | category | flops | bytes accessed | tf_op | source)
XLA Modules:
  0.0 407.7 jit_solution(6416141053726972275)
XLA Ops:
  3.3 10.6 %collective-permute-start.1 = (f32[1,32,128]{2,1,0:T(8,128)S(1)}, f32[1,32,128]{2,1,0:T(8,128)S(1)}, u32[]{:S(2)}, u32[]{:S(2)}) collective-permute-start(f32[1,32,128]{2,1,0:T(8,128)S(1)} %copy.418), channel_id=1, source_target_pairs={{32,0},{64,32},{96,64},{128,96},{160,128},{192,160},{224,192},{256... | collective-permute-start | bytes 49160 | tf_op jit(solution)/shard_map/ppermute | solution.py:20
  16.8 2.2 collective-permute-start.2
  19.0 6.1 %collective-permute-start.3 = (f32[1,32,128]{2,1,0:T(8,128)S(1)}, f32[1,32,128]{2,1,0:T(8,128)S(1)}, u32[]{:S(2)}, u32[]{:S(2)}) collective-permute-start(f32[1,32,128]{2,1,0:T(8,128)S(1)} %get-tuple-element.52), channel_id=1, source_target_pairs={{32,0},{64,32},{96,64},{128,96},{160,128},{192,160},{224,192},{256... | collective-permute-start | bytes 49160 | tf_op jit(solution)/shard_map/ppermute | solution.py:20
  28.7 2.1 collective-permute-start.5
  30.8 3.2 collective-permute-start.4
  34.1 2.1 collective-permute-start.7
  36.2 3.2 collective-permute-start.6
  39.8 4.5 %collective-permute-start.9 = (f32[18,34,1]{2,1,0:T(8,128)S(1)}, f32[18,34,1]{2,1,0:T(8,128)S(1)}, u32[]{:S(2)}, u32[]{:S(2)}) collective-permute-start(f32[18,34,1]{2,1,0:T(8,128)S(1)} %get-tuple-element.31), channel_id=1, source_target_pairs={{8,0},{16,8},{24,16},{9,1},{17,9},{25,17},{10,2},{18,10},{26,18},{... | collective-permute-start | bytes 7352 | tf_op jit(solution)/shard_map/ppermute | solution.py:20
  44.3 3.0 collective-permute-start.8
  49.5 3.8 collective-permute-start.10
  53.7 2.7 collective-permute-done.11
  58.8 10.1 %reshape.196 = f32[4,4,8,4,32,4]{5,4,3,2,1,0:T(8,128)} reshape(f32[16,32,128]{2,1,0:T(8,128)S(1)} %get-tuple-element.19) | data formatting | bytes 524288 | tf_op jit(solution)/shard_map/reshape | solution.py:100
  68.9 5.9 %copy.426 = f32[4,4,8,4,32,4]{4,1,5,3,2,0:T(4,128)S(1)} copy(f32[4,4,8,4,32,4]{5,4,3,2,1,0:T(8,128)} %reshape.196) | data formatting | bytes 524288 | tf_op jit(solution)/shard_map/reshape | solution.py:100
  82.5 4.1 %all-to-all-start = ((bf16[4,2,1024]{2,1,0:T(2,128)(2,1)}), bf16[4,2,1024]{2,1,0:T(2,128)(2,1)S(1)}, u32[]{:S(2)}, u32[]{:S(2)}) async-start(bf16[4,2,1024]{2,1,0:T(2,128)(2,1)} %reshape.214), calls=%async_computation | async-start | bytes 32768 | tf_op jit(solution)/shard_map/all_to_all | solution.py:139
  86.6 3.1 all-to-all-done
  92.7 7.2 %all-to-all-start.1 = ((bf16[8,2,512]{2,1,0:T(2,128)(2,1)}), bf16[8,2,512]{2,1,0:T(2,128)(2,1)S(1)}, u32[]{:S(2)}, u32[]{:S(2)}) async-start(bf16[8,2,512]{2,1,0:T(2,128)(2,1)} %reshape.216), calls=%async_computation.1 | async-start | bytes 32768 | tf_op jit(solution)/shard_map/all_to_all | solution.py:143
  101.3 4.1 %all-to-all-done.1 = bf16[8,2,512]{2,1,0:T(2,128)(2,1)S(1)} async-done(((bf16[8,2,512]{2,1,0:T(2,128)(2,1)}), bf16[8,2,512]{2,1,0:T(2,128)(2,1)S(1)}, u32[]{:S(2)}, u32[]{:S(2)}) %all-to-all-start.1) | async-done | bytes 16416 | tf_op jit(solution)/shard_map/all_to_all | solution.py:143
  106.8 9.5 %all-to-all-start.2 = ((bf16[2,128,32]{2,0,1:T(2,128)(2,1)}), bf16[2,128,32]{2,0,1:T(2,128)(2,1)S(1)}, u32[]{:S(2)}, u32[]{:S(2)}) async-start(bf16[2,128,32]{2,0,1:T(2,128)(2,1)} %copy.434), calls=%async_computation.2 | async-start | bytes 131072 | tf_op jit(solution)/shard_map/all_to_all | solution.py:149
  116.4 5.2 %collective-permute-start.13 = (f32[1,32,128]{2,1,0:T(8,128)S(1)}, f32[1,32,128]{2,1,0:T(8,128)S(1)}, u32[]{:S(2)}, u32[]{:S(2)}) collective-permute-start(f32[1,32,128]{2,1,0:T(8,128)S(1)} %get-tuple-element.51), channel_id=1, source_target_pairs={{32,0},{64,32},{96,64},{128,96},{160,128},{192,160},{224,192},{256... | collective-permute-start | bytes 49160 | tf_op jit(solution)/shard_map/ppermute | solution.py:20
  121.6 2.3 collective-permute-start.12
  127.7 9.0 %all-to-all-start.3 = ((bf16[128,2,32]{2,1,0:T(2,128)(2,1)}), bf16[128,2,32]{2,1,0:T(2,128)(2,1)S(1)}, u32[]{:S(2)}, u32[]{:S(2)}) async-start(bf16[128,2,32]{2,1,0:T(2,128)(2,1)} %copy.438), calls=%async_computation.3 | async-start | bytes 131072 | tf_op jit(solution)/shard_map/all_to_all | solution.py:172
  136.8 3.0 collective-permute-start.15
  139.9 2.2 collective-permute-start.14
  142.2 3.5 all-to-all-done.3
  147.0 4.4 %all-to-all-start.4 = ((bf16[8,2,512]{2,1,0:T(2,128)(2,1)}), bf16[8,2,512]{2,1,0:T(2,128)(2,1)S(1)}, u32[]{:S(2)}, u32[]{:S(2)}) async-start(bf16[8,2,512]{2,1,0:T(2,128)(2,1)} %reshape.218), calls=%async_computation.4 | async-start | bytes 32768 | tf_op jit(solution)/shard_map/all_to_all | solution.py:176
  151.4 5.6 %all-to-all-done.4 = bf16[8,2,512]{2,1,0:T(2,128)(2,1)S(1)} async-done(((bf16[8,2,512]{2,1,0:T(2,128)(2,1)}), bf16[8,2,512]{2,1,0:T(2,128)(2,1)S(1)}, u32[]{:S(2)}, u32[]{:S(2)}) %all-to-all-start.4) | async-done | bytes 16416 | tf_op jit(solution)/shard_map/all_to_all | solution.py:176
  160.0 4.6 %all-to-all-start.5 = ((bf16[4,2,1024]{2,1,0:T(2,128)(2,1)}), bf16[4,2,1024]{2,1,0:T(2,128)(2,1)S(1)}, u32[]{:S(2)}, u32[]{:S(2)}) async-start(bf16[4,2,1024]{2,1,0:T(2,128)(2,1)} %reshape.220), calls=%async_computation.5 | async-start | bytes 32768 | tf_op jit(solution)/shard_map/all_to_all | solution.py:178
  167.6 3.6 collective-permute-start.16
  174.7 15.5 %fusion.9 = f32[4,4,8,4,32,4]{5,4,3,2,1,0:T(8,128)} fusion(f32[4,2,1,1,1,1]{0,1,5,4,3,2:T(2,128)S(1)} %copy-done.13, f32[4,4,8,4,32,2]{4,3,5,2,1,0:T(4,128)S(1)} %convolution_bitcast_fusion.2), kind=kOutput, calls=%fused_computation.37 | convolution fusion | flops 1572864 | bytes 393248 | tf_op jit(solution)/shard_map/kc,pizjyc->pizjyk/dot_general | solution.py:114
  190.2 8.2 %reshape.198 = f32[16,32,128]{2,1,0:T(8,128)S(1)} reshape(f32[4,4,8,4,32,4]{5,4,3,2,1,0:T(8,128)} %fusion.9) | data formatting | bytes 524288 | tf_op jit(solution)/shard_map/reshape | solution.py:115
  200.0 3.3 collective-permute-start.19
  203.3 2.8 collective-permute-start.18
  206.2 4.6 %collective-permute-done.18 = f32[1,32,128]{2,1,0:T(8,128)S(1)} collective-permute-done((f32[1,32,128]{2,1,0:T(8,128)S(1)}, f32[1,32,128]{2,1,0:T(8,128)S(1)}, u32[]{:S(2)}, u32[]{:S(2)}) %collective-permute-start.18) | collective-permute-done | bytes 16416 | tf_op jit(solution)/shard_map/ppermute | solution.py:19
  210.8 3.0 collective-permute-start.21
  213.9 2.4 collective-permute-start.20
  218.5 4.3 %collective-permute-start.23 = (f32[18,34,1]{2,1,0:T(8,128)S(1)}, f32[18,34,1]{2,1,0:T(8,128)S(1)}, u32[]{:S(2)}, u32[]{:S(2)}) collective-permute-start(f32[18,34,1]{2,1,0:T(8,128)S(1)} %get-tuple-element.25), channel_id=1, source_target_pairs={{8,0},{16,8},{24,16},{9,1},{17,9},{25,17},{10,2},{18,10},{26,18},{... | collective-permute-start | bytes 7352 | tf_op jit(solution)/shard_map/ppermute | solution.py:20
  222.8 3.5 collective-permute-start.22
  226.3 3.3 collective-permute-done.23
  232.9 10.1 %reshape.199 = f32[4,4,8,4,32,4]{5,4,3,2,1,0:T(8,128)} reshape(f32[16,32,128]{2,1,0:T(8,128)S(1)} %get-tuple-element.16) | data formatting | bytes 524288 | tf_op jit(solution)/shard_map/reshape | solution.py:100
  243.0 5.9 %copy.454 = f32[4,4,8,4,32,4]{4,1,5,3,2,0:T(4,128)S(1)} copy(f32[4,4,8,4,32,4]{5,4,3,2,1,0:T(8,128)} %reshape.199) | data formatting | bytes 524288 | tf_op jit(solution)/shard_map/reshape | solution.py:100
  256.8 7.1 %all_to_all.210 = bf16[4,2,1024]{2,1,0:T(2,128)(2,1)S(1)} all-to-all(bf16[4,2,1024]{2,1,0:T(2,128)(2,1)S(1)} %reshape.222), channel_id=1, replica_groups=mesh['bx'=16,'by'=4,'bz'=8] {'by'}, dimensions={0} | all-to-all | bytes 32768 | tf_op jit(solution)/shard_map/all_to_all | solution.py:139
  266.2 10.5 %all_to_all.211 = bf16[8,2,512]{2,1,0:T(2,128)(2,1)S(1)} all-to-all(bf16[8,2,512]{2,1,0:T(2,128)(2,1)S(1)} %reshape.224), channel_id=1, replica_groups=mesh['bx'=16,'by'=4,'bz'=8] {'bz'}, dimensions={0} | all-to-all | bytes 32768 | tf_op jit(solution)/shard_map/all_to_all | solution.py:143
  278.9 7.7 %all-to-all-start.8 = ((bf16[2,128,32]{2,0,1:T(2,128)(2,1)}), bf16[2,128,32]{2,0,1:T(2,128)(2,1)S(1)}, u32[]{:S(2)}, u32[]{:S(2)}) async-start(bf16[2,128,32]{2,0,1:T(2,128)(2,1)} %copy.462), calls=%async_computation.8 | async-start | bytes 131072 | tf_op jit(solution)/shard_map/all_to_all | solution.py:149
  286.6 5.2 %collective-permute-start.25 = (f32[1,32,128]{2,1,0:T(8,128)S(1)}, f32[1,32,128]{2,1,0:T(8,128)S(1)}, u32[]{:S(2)}, u32[]{:S(2)}) collective-permute-start(f32[1,32,128]{2,1,0:T(8,128)S(1)} %get-tuple-element.47), channel_id=1, source_target_pairs={{32,0},{64,32},{96,64},{128,96},{160,128},{192,160},{224,192},{256... | collective-permute-start | bytes 49160 | tf_op jit(solution)/shard_map/ppermute | solution.py:20
  299.3 8.6 %all-to-all-start.9 = ((bf16[128,2,32]{2,1,0:T(2,128)(2,1)}), bf16[128,2,32]{2,1,0:T(2,128)(2,1)S(1)}, u32[]{:S(2)}, u32[]{:S(2)}) async-start(bf16[128,2,32]{2,1,0:T(2,128)(2,1)} %copy.466), calls=%async_computation.9 | async-start | bytes 131072 | tf_op jit(solution)/shard_map/all_to_all | solution.py:172
  308.0 3.0 collective-permute-start.27
  311.0 2.2 collective-permute-start.26
  313.3 3.5 all-to-all-done.9
  318.8 4.4 %all-to-all-start.10 = ((bf16[8,2,512]{2,1,0:T(2,128)(2,1)}), bf16[8,2,512]{2,1,0:T(2,128)(2,1)S(1)}, u32[]{:S(2)}, u32[]{:S(2)}) async-start(bf16[8,2,512]{2,1,0:T(2,128)(2,1)} %reshape.226), calls=%async_computation.10 | async-start | bytes 32768 | tf_op jit(solution)/shard_map/all_to_all | solution.py:176
  323.8 5.0 %all-to-all-done.10 = bf16[8,2,512]{2,1,0:T(2,128)(2,1)S(1)} async-done(((bf16[8,2,512]{2,1,0:T(2,128)(2,1)}), bf16[8,2,512]{2,1,0:T(2,128)(2,1)S(1)}, u32[]{:S(2)}, u32[]{:S(2)}) %all-to-all-start.10) | async-done | bytes 16416 | tf_op jit(solution)/shard_map/all_to_all | solution.py:176
  331.8 4.6 %all-to-all-start.11 = ((bf16[4,2,1024]{2,1,0:T(2,128)(2,1)}), bf16[4,2,1024]{2,1,0:T(2,128)(2,1)S(1)}, u32[]{:S(2)}, u32[]{:S(2)}) async-start(bf16[4,2,1024]{2,1,0:T(2,128)(2,1)} %reshape.228), calls=%async_computation.11 | async-start | bytes 32768 | tf_op jit(solution)/shard_map/all_to_all | solution.py:178
  339.3 3.8 collective-permute-start.28
  348.0 16.2 %fusion.6 = f32[4,4,8,4,32,4]{5,4,3,2,1,0:T(8,128)} fusion(f32[4,2,1,1,1,1]{0,1,5,4,3,2:T(2,128)} %constant.103, f32[4,4,8,4,32,2]{4,3,5,2,1,0:T(4,128)S(1)} %convolution_bitcast_fusion), kind=kOutput, calls=%fused_computation.34 | convolution fusion | flops 1572864 | bytes 393248 | tf_op jit(solution)/shard_map/kc,pizjyc->pizjyk/dot_general | solution.py:114
  364.3 8.8 %reshape.201 = f32[16,32,128]{2,1,0:T(8,128)} reshape(f32[4,4,8,4,32,4]{5,4,3,2,1,0:T(8,128)} %fusion.6) | data formatting | bytes 524288 | tf_op jit(solution)/shard_map/reshape | solution.py:115
  373.1 2.3 fusion.45
  375.5 3.3 collective-permute-start.31
  378.9 2.8 collective-permute-start.30
  381.7 4.6 %collective-permute-done.30 = f32[1,32,128]{2,1,0:T(8,128)S(1)} collective-permute-done((f32[1,32,128]{2,1,0:T(8,128)S(1)}, f32[1,32,128]{2,1,0:T(8,128)S(1)}, u32[]{:S(2)}, u32[]{:S(2)}) %collective-permute-start.30) | collective-permute-done | bytes 16416 | tf_op jit(solution)/shard_map/ppermute | solution.py:19
  386.4 3.0 collective-permute-start.33
  389.4 2.2 collective-permute-start.32
  391.7 2.1 collective-permute-done.32
  394.1 4.3 %collective-permute-start.35 = (f32[18,34,1]{2,1,0:T(8,128)S(1)}, f32[18,34,1]{2,1,0:T(8,128)S(1)}, u32[]{:S(2)}, u32[]{:S(2)}) collective-permute-start(f32[18,34,1]{2,1,0:T(8,128)S(1)} %get-tuple-element.21), channel_id=1, source_target_pairs={{8,0},{16,8},{24,16},{9,1},{17,9},{25,17},{10,2},{18,10},{26,18},{... | collective-permute-start | bytes 7352 | tf_op jit(solution)/shard_map/ppermute | solution.py:20
  398.4 3.5 collective-permute-start.34
  401.9 3.3 collective-permute-done.35
  (232 shorter events, 83.7 us)
Async XLA Ops:
  0.6 33.4 %copy-start.1 = (f32[16,32,128]{2,1,0:T(8,128)S(1)}, f32[16,32,128]{2,1,0:T(8,128)}, u32[]{:S(2)}) copy-start(f32[16,32,128]{2,1,0:T(8,128)} %param.9) | copy-start | bytes 786436
  3.3 25.4 %collective-permute-start.1 = (f32[1,32,128]{2,1,0:T(8,128)S(1)}, f32[1,32,128]{2,1,0:T(8,128)S(1)}, u32[]{:S(2)}, u32[]{:S(2)}) collective-permute-start(f32[1,32,128]{2,1,0:T(8,128)S(1)} %copy.418), channel_id=1, source_target_pairs={{32,0},{64,32},{96,64},{128,96},{160,128},{192,160},{224,192},{256... | collective-permute-start | bytes 49160 | tf_op jit(solution)/shard_map/ppermute | solution.py:20
  14.1 14.6 %collective-permute-start = (f32[1,32,128]{2,1,0:T(8,128)S(1)}, f32[1,32,128]{2,1,0:T(8,128)S(1)}, u32[]{:S(2)}, u32[]{:S(2)}) collective-permute-start(f32[1,32,128]{2,1,0:T(8,128)S(1)} %copy.414), channel_id=1, source_target_pairs={{0,32},{32,64},{64,96},{96,128},{128,160},{160,192},{192,224},{224... | collective-permute-start | bytes 49160 | tf_op jit(solution)/shard_map/ppermute | solution.py:19
  16.8 17.2 %collective-permute-start.2 = (f32[1,32,128]{2,1,0:T(8,128)S(1)}, f32[1,32,128]{2,1,0:T(8,128)S(1)}, u32[]{:S(2)}, u32[]{:S(2)}) collective-permute-start(f32[1,32,128]{2,1,0:T(8,128)S(1)} %get-tuple-element.53), channel_id=1, source_target_pairs={{0,32},{32,64},{64,96},{96,128},{128,160},{160,192},{192,224},{224... | collective-permute-start | bytes 49160 | tf_op jit(solution)/shard_map/ppermute | solution.py:19
  19.0 15.1 %collective-permute-start.3 = (f32[1,32,128]{2,1,0:T(8,128)S(1)}, f32[1,32,128]{2,1,0:T(8,128)S(1)}, u32[]{:S(2)}, u32[]{:S(2)}) collective-permute-start(f32[1,32,128]{2,1,0:T(8,128)S(1)} %get-tuple-element.52), channel_id=1, source_target_pairs={{32,0},{64,32},{96,64},{128,96},{160,128},{192,160},{224,192},{256... | collective-permute-start | bytes 49160 | tf_op jit(solution)/shard_map/ppermute | solution.py:20
  26.8 30.8 %copy-start.6 = (f32[16,32,128]{2,1,0:T(8,128)S(1)}, f32[16,32,128]{2,1,0:T(8,128)}, u32[]{:S(2)}) copy-start(f32[16,32,128]{2,1,0:T(8,128)} %param.8) | copy-start | bytes 786436
  28.7 10.8 %collective-permute-start.5 = (f32[18,1,128]{2,1,0:T(1,128)S(1)}, f32[18,1,128]{2,1,0:T(1,128)S(1)}, u32[]{:S(2)}, u32[]{:S(2)}) collective-permute-start(f32[18,1,128]{2,1,0:T(1,128)S(1)} %get-tuple-element.43), channel_id=1, source_target_pairs={{1,0},{2,1},{3,2},{4,3},{5,4},{6,5},{7,6},{9,8},{10,9},{11,10},{12... | collective-permute-start | bytes 27656 | tf_op jit(solution)/shard_map/ppermute | solution.py:20
  30.8 8.7 %collective-permute-start.4 = (f32[18,1,128]{2,1,0:T(1,128)S(1)}, f32[18,1,128]{2,1,0:T(1,128)S(1)}, u32[]{:S(2)}, u32[]{:S(2)}) collective-permute-start(f32[18,1,128]{2,1,0:T(1,128)S(1)} %get-tuple-element.42), channel_id=1, source_target_pairs={{0,1},{1,2},{2,3},{3,4},{4,5},{5,6},{6,7},{8,9},{9,10},{10,11},{11... | collective-permute-start | bytes 27656 | tf_op jit(solution)/shard_map/ppermute | solution.py:19
  34.1 13.2 %collective-permute-start.7 = (f32[18,1,128]{2,1,0:T(1,128)S(1)}, f32[18,1,128]{2,1,0:T(1,128)S(1)}, u32[]{:S(2)}, u32[]{:S(2)}) collective-permute-start(f32[18,1,128]{2,1,0:T(1,128)S(1)} %get-tuple-element.41), channel_id=1, source_target_pairs={{1,0},{2,1},{3,2},{4,3},{5,4},{6,5},{7,6},{9,8},{10,9},{11,10},{12... | collective-permute-start | bytes 27656 | tf_op jit(solution)/shard_map/ppermute | solution.py:20
  36.2 11.1 %collective-permute-start.6 = (f32[18,1,128]{2,1,0:T(1,128)S(1)}, f32[18,1,128]{2,1,0:T(1,128)S(1)}, u32[]{:S(2)}, u32[]{:S(2)}) collective-permute-start(f32[18,1,128]{2,1,0:T(1,128)S(1)} %get-tuple-element.40), channel_id=1, source_target_pairs={{0,1},{1,2},{2,3},{3,4},{4,5},{5,6},{6,7},{8,9},{9,10},{10,11},{11... | collective-permute-start | bytes 27656 | tf_op jit(solution)/shard_map/ppermute | solution.py:19
  39.8 13.7 %collective-permute-start.9 = (f32[18,34,1]{2,1,0:T(8,128)S(1)}, f32[18,34,1]{2,1,0:T(8,128)S(1)}, u32[]{:S(2)}, u32[]{:S(2)}) collective-permute-start(f32[18,34,1]{2,1,0:T(8,128)S(1)} %get-tuple-element.31), channel_id=1, source_target_pairs={{8,0},{16,8},{24,16},{9,1},{17,9},{25,17},{10,2},{18,10},{26,18},{... | collective-permute-start | bytes 7352 | tf_op jit(solution)/shard_map/ppermute | solution.py:20
  44.3 9.1 %collective-permute-start.8 = (f32[18,34,1]{2,1,0:T(8,128)S(1)}, f32[18,34,1]{2,1,0:T(8,128)S(1)}, u32[]{:S(2)}, u32[]{:S(2)}) collective-permute-start(f32[18,34,1]{2,1,0:T(8,128)S(1)} %get-tuple-element.30), channel_id=1, source_target_pairs={{0,8},{8,16},{16,24},{1,9},{9,17},{17,25},{2,10},{10,18},{18,26},{... | collective-permute-start | bytes 7352 | tf_op jit(solution)/shard_map/ppermute | solution.py:19
  47.6 8.8 %collective-permute-start.11 = (f32[18,34,1]{2,1,0:T(8,128)S(1)}, f32[18,34,1]{2,1,0:T(8,128)S(1)}, u32[]{:S(2)}, u32[]{:S(2)}) collective-permute-start(f32[18,34,1]{2,1,0:T(8,128)S(1)} %get-tuple-element.29), channel_id=1, source_target_pairs={{8,0},{16,8},{24,16},{9,1},{17,9},{25,17},{10,2},{18,10},{26,18},{... | collective-permute-start | bytes 7352 | tf_op jit(solution)/shard_map/ppermute | solution.py:20
  49.5 8.1 %collective-permute-start.10 = (f32[18,34,1]{2,1,0:T(8,128)S(1)}, f32[18,34,1]{2,1,0:T(8,128)S(1)}, u32[]{:S(2)}, u32[]{:S(2)}) collective-permute-start(f32[18,34,1]{2,1,0:T(8,128)S(1)} %get-tuple-element.28), channel_id=1, source_target_pairs={{0,8},{8,16},{16,24},{1,9},{9,17},{17,25},{2,10},{10,18},{18,26},{... | collective-permute-start | bytes 7352 | tf_op jit(solution)/shard_map/ppermute | solution.py:19
  58.8 139.6 %copy-start.2 = (f32[16,32,128]{2,1,0:T(8,128)}, f32[16,32,128]{2,1,0:T(8,128)S(1)}, u32[]{:S(2)}) copy-start(f32[16,32,128]{2,1,0:T(8,128)S(1)} %get-tuple-element.19) | copy-start | bytes 786436
  58.8 16.0 %copy-start.16 = (f32[2,4,1,1,1,1]{1,0,5,4,3,2:T(2,128)S(1)}, f32[2,4,1,1,1,1]{1,0,5,4,3,2:T(2,128)}, u32[]{:S(2)}) copy-start(f32[2,4,1,1,1,1]{1,0,5,4,3,2:T(2,128)} %constant.102) | copy-start | bytes 100
  79.8 93.3 %copy-start.13 = (f32[4,2,1,1,1,1]{0,1,5,4,3,2:T(2,128)S(1)}, f32[4,2,1,1,1,1]{0,1,5,4,3,2:T(2,128)}, u32[]{:S(2)}) copy-start(f32[4,2,1,1,1,1]{0,1,5,4,3,2:T(2,128)} %constant.103) | copy-start | bytes 100
  82.5 7.3 %all-to-all-start = ((bf16[4,2,1024]{2,1,0:T(2,128)(2,1)}), bf16[4,2,1024]{2,1,0:T(2,128)(2,1)S(1)}, u32[]{:S(2)}, u32[]{:S(2)}) async-start(bf16[4,2,1024]{2,1,0:T(2,128)(2,1)} %reshape.214), calls=%async_computation | async-start | bytes 32768 | tf_op jit(solution)/shard_map/all_to_all | solution.py:139
  86.6 64.7 %copy-start.19 = (s32[128]{0:T(128)}, s32[128]{0:T(128)S(1)}, u32[]{:S(2)}) copy-start(s32[128]{0:T(128)S(1)} %iota_add_fusion.1) | copy-start | bytes 1540
  92.7 12.7 %all-to-all-start.1 = ((bf16[8,2,512]{2,1,0:T(2,128)(2,1)}), bf16[8,2,512]{2,1,0:T(2,128)(2,1)S(1)}, u32[]{:S(2)}, u32[]{:S(2)}) async-start(bf16[8,2,512]{2,1,0:T(2,128)(2,1)} %reshape.216), calls=%async_computation.1 | async-start | bytes 32768 | tf_op jit(solution)/shard_map/all_to_all | solution.py:143
  99.9 40.0 %copy-start.18 = (f32[32]{0:T(128)}, f32[32]{0:T(128)S(1)}, u32[]{:S(2)}) copy-start(f32[32]{0:T(128)S(1)} %multiply_subtract_fusion) | copy-start | bytes 388
  106.8 18.4 %all-to-all-start.2 = ((bf16[2,128,32]{2,0,1:T(2,128)(2,1)}), bf16[2,128,32]{2,0,1:T(2,128)(2,1)S(1)}, u32[]{:S(2)}, u32[]{:S(2)}) async-start(bf16[2,128,32]{2,0,1:T(2,128)(2,1)} %copy.434), calls=%async_computation.2 | async-start | bytes 131072 | tf_op jit(solution)/shard_map/all_to_all | solution.py:149
  116.4 20.4 %collective-permute-start.13 = (f32[1,32,128]{2,1,0:T(8,128)S(1)}, f32[1,32,128]{2,1,0:T(8,128)S(1)}, u32[]{:S(2)}, u32[]{:S(2)}) collective-permute-start(f32[1,32,128]{2,1,0:T(8,128)S(1)} %get-tuple-element.51), channel_id=1, source_target_pairs={{32,0},{64,32},{96,64},{128,96},{160,128},{192,160},{224,192},{256... | collective-permute-start | bytes 49160 | tf_op jit(solution)/shard_map/ppermute | solution.py:20
  121.6 15.2 %collective-permute-start.12 = (f32[1,32,128]{2,1,0:T(8,128)S(1)}, f32[1,32,128]{2,1,0:T(8,128)S(1)}, u32[]{:S(2)}, u32[]{:S(2)}) collective-permute-start(f32[1,32,128]{2,1,0:T(8,128)S(1)} %get-tuple-element.50), channel_id=1, source_target_pairs={{0,32},{32,64},{64,96},{96,128},{128,160},{160,192},{192,224},{224... | collective-permute-start | bytes 49160 | tf_op jit(solution)/shard_map/ppermute | solution.py:19
  127.7 17.9 %all-to-all-start.3 = ((bf16[128,2,32]{2,1,0:T(2,128)(2,1)}), bf16[128,2,32]{2,1,0:T(2,128)(2,1)S(1)}, u32[]{:S(2)}, u32[]{:S(2)}) async-start(bf16[128,2,32]{2,1,0:T(2,128)(2,1)} %copy.438), calls=%async_computation.3 | async-start | bytes 131072 | tf_op jit(solution)/shard_map/all_to_all | solution.py:172
  136.8 14.5 %collective-permute-start.15 = (f32[18,1,128]{2,1,0:T(1,128)S(1)}, f32[18,1,128]{2,1,0:T(1,128)S(1)}, u32[]{:S(2)}, u32[]{:S(2)}) collective-permute-start(f32[18,1,128]{2,1,0:T(1,128)S(1)} %get-tuple-element.39), channel_id=1, source_target_pairs={{1,0},{2,1},{3,2},{4,3},{5,4},{6,5},{7,6},{9,8},{10,9},{11,10},{12... | collective-permute-start | bytes 27656 | tf_op jit(solution)/shard_map/ppermute | solution.py:20
  139.9 11.5 %collective-permute-start.14 = (f32[18,1,128]{2,1,0:T(1,128)S(1)}, f32[18,1,128]{2,1,0:T(1,128)S(1)}, u32[]{:S(2)}, u32[]{:S(2)}) collective-permute-start(f32[18,1,128]{2,1,0:T(1,128)S(1)} %get-tuple-element.38), channel_id=1, source_target_pairs={{0,1},{1,2},{2,3},{3,4},{4,5},{5,6},{6,7},{8,9},{9,10},{10,11},{11... | collective-permute-start | bytes 27656 | tf_op jit(solution)/shard_map/ppermute | solution.py:19
  147.0 10.0 %all-to-all-start.4 = ((bf16[8,2,512]{2,1,0:T(2,128)(2,1)}), bf16[8,2,512]{2,1,0:T(2,128)(2,1)S(1)}, u32[]{:S(2)}, u32[]{:S(2)}) async-start(bf16[8,2,512]{2,1,0:T(2,128)(2,1)} %reshape.218), calls=%async_computation.4 | async-start | bytes 32768 | tf_op jit(solution)/shard_map/all_to_all | solution.py:176
  151.4 47.0 %copy-start.11 = (f32[18,1,128]{2,1,0:T(1,128)}, f32[18,1,128]{2,1,0:T(1,128)S(1)}, u32[]{:S(2)}) copy-start(f32[18,1,128]{2,1,0:T(1,128)S(1)} %collective-permute-done.15) | copy-start | bytes 27652
  151.4 47.0 %copy-start.12 = (f32[18,1,128]{2,1,0:T(1,128)}, f32[18,1,128]{2,1,0:T(1,128)S(1)}, u32[]{:S(2)}) copy-start(f32[18,1,128]{2,1,0:T(1,128)S(1)} %collective-permute-done.14) | copy-start | bytes 27652
  160.0 11.2 %all-to-all-start.5 = ((bf16[4,2,1024]{2,1,0:T(2,128)(2,1)}), bf16[4,2,1024]{2,1,0:T(2,128)(2,1)S(1)}, u32[]{:S(2)}, u32[]{:S(2)}) async-start(bf16[4,2,1024]{2,1,0:T(2,128)(2,1)} %reshape.220), calls=%async_computation.5 | async-start | bytes 32768 | tf_op jit(solution)/shard_map/all_to_all | solution.py:178
  165.6 32.7 %collective-permute-start.17 = (f32[18,34,1]{2,1,0:T(8,128)}, f32[18,34,1]{2,1,0:T(8,128)}, u32[]{:S(2)}, u32[]{:S(2)}) collective-permute-start(f32[18,34,1]{2,1,0:T(8,128)} %get-tuple-element.27), channel_id=1, source_target_pairs={{8,0},{16,8},{24,16},{9,1},{17,9},{25,17},{10,2},{18,10},{26,18},{... | collective-permute-start | bytes 7352 | tf_op jit(solution)/shard_map/ppermute | solution.py:20
  167.6 30.8 %collective-permute-start.16 = (f32[18,34,1]{2,1,0:T(8,128)}, f32[18,34,1]{2,1,0:T(8,128)}, u32[]{:S(2)}, u32[]{:S(2)}) collective-permute-start(f32[18,34,1]{2,1,0:T(8,128)} %get-tuple-element.26), channel_id=1, source_target_pairs={{0,8},{8,16},{16,24},{1,9},{9,17},{17,25},{2,10},{10,18},{18,26},{... | collective-permute-start | bytes 7352 | tf_op jit(solution)/shard_map/ppermute | solution.py:19
  174.7 23.7 %copy-start.4 = (f32[16,32,128]{2,1,0:T(8,128)S(1)}, f32[16,32,128]{2,1,0:T(8,128)}, u32[]{:S(2)}) copy-start(f32[16,32,128]{2,1,0:T(8,128)} %get-tuple-element.18) | copy-start | bytes 786436
  198.3 31.3 %copy-start.8 = (f32[16,32,128]{2,1,0:T(8,128)}, f32[16,32,128]{2,1,0:T(8,128)S(1)}, u32[]{:S(2)}) copy-start(f32[16,32,128]{2,1,0:T(8,128)S(1)} %reshape.198) | copy-start | bytes 786436
  200.0 6.2 %collective-permute-start.19 = (f32[1,32,128]{2,1,0:T(8,128)S(1)}, f32[1,32,128]{2,1,0:T(8,128)S(1)}, u32[]{:S(2)}, u32[]{:S(2)}) collective-permute-start(f32[1,32,128]{2,1,0:T(8,128)S(1)} %get-tuple-element.49), channel_id=1, source_target_pairs={{32,0},{64,32},{96,64},{128,96},{160,128},{192,160},{224,192},{256... | collective-permute-start | bytes 49160 | tf_op jit(solution)/shard_map/ppermute | solution.py:20
  203.3 7.5 %collective-permute-start.18 = (f32[1,32,128]{2,1,0:T(8,128)S(1)}, f32[1,32,128]{2,1,0:T(8,128)S(1)}, u32[]{:S(2)}, u32[]{:S(2)}) collective-permute-start(f32[1,32,128]{2,1,0:T(8,128)S(1)} %get-tuple-element.48), channel_id=1, source_target_pairs={{0,32},{32,64},{64,96},{96,128},{128,160},{160,192},{192,224},{224... | collective-permute-start | bytes 49160 | tf_op jit(solution)/shard_map/ppermute | solution.py:19
  210.8 5.5 %collective-permute-start.21 = (f32[18,1,128]{2,1,0:T(1,128)S(1)}, f32[18,1,128]{2,1,0:T(1,128)S(1)}, u32[]{:S(2)}, u32[]{:S(2)}) collective-permute-start(f32[18,1,128]{2,1,0:T(1,128)S(1)} %get-tuple-element.37), channel_id=1, source_target_pairs={{1,0},{2,1},{3,2},{4,3},{5,4},{6,5},{7,6},{9,8},{10,9},{11,10},{12... | collective-permute-start | bytes 27656 | tf_op jit(solution)/shard_map/ppermute | solution.py:20
  213.9 4.4 %collective-permute-start.20 = (f32[18,1,128]{2,1,0:T(1,128)S(1)}, f32[18,1,128]{2,1,0:T(1,128)S(1)}, u32[]{:S(2)}, u32[]{:S(2)}) collective-permute-start(f32[18,1,128]{2,1,0:T(1,128)S(1)} %get-tuple-element.36), channel_id=1, source_target_pairs={{0,1},{1,2},{2,3},{3,4},{4,5},{5,6},{6,7},{8,9},{9,10},{10,11},{11... | collective-permute-start | bytes 27656 | tf_op jit(solution)/shard_map/ppermute | solution.py:19
  218.5 11.1 %collective-permute-start.23 = (f32[18,34,1]{2,1,0:T(8,128)S(1)}, f32[18,34,1]{2,1,0:T(8,128)S(1)}, u32[]{:S(2)}, u32[]{:S(2)}) collective-permute-start(f32[18,34,1]{2,1,0:T(8,128)S(1)} %get-tuple-element.25), channel_id=1, source_target_pairs={{8,0},{16,8},{24,16},{9,1},{17,9},{25,17},{10,2},{18,10},{26,18},{... | collective-permute-start | bytes 7352 | tf_op jit(solution)/shard_map/ppermute | solution.py:20
  222.8 8.0 %collective-permute-start.22 = (f32[18,34,1]{2,1,0:T(8,128)S(1)}, f32[18,34,1]{2,1,0:T(8,128)S(1)}, u32[]{:S(2)}, u32[]{:S(2)}) collective-permute-start(f32[18,34,1]{2,1,0:T(8,128)S(1)} %get-tuple-element.24), channel_id=1, source_target_pairs={{0,8},{8,16},{16,24},{1,9},{9,17},{17,25},{2,10},{10,18},{18,26},{... | collective-permute-start | bytes 7352 | tf_op jit(solution)/shard_map/ppermute | solution.py:19
  232.2 0.7 copy-start.10
  232.9 16.0 %copy-start.17 = (f32[2,4,1,1,1,1]{1,0,5,4,3,2:T(2,128)S(1)}, f32[2,4,1,1,1,1]{1,0,5,4,3,2:T(2,128)}, u32[]{:S(2)}) copy-start(f32[2,4,1,1,1,1]{1,0,5,4,3,2:T(2,128)} %constant.102) | copy-start | bytes 100
  278.9 16.5 %all-to-all-start.8 = ((bf16[2,128,32]{2,0,1:T(2,128)(2,1)}), bf16[2,128,32]{2,0,1:T(2,128)(2,1)S(1)}, u32[]{:S(2)}, u32[]{:S(2)}) async-start(bf16[2,128,32]{2,0,1:T(2,128)(2,1)} %copy.462), calls=%async_computation.8 | async-start | bytes 131072 | tf_op jit(solution)/shard_map/all_to_all | solution.py:149
  286.6 21.4 %collective-permute-start.25 = (f32[1,32,128]{2,1,0:T(8,128)S(1)}, f32[1,32,128]{2,1,0:T(8,128)S(1)}, u32[]{:S(2)}, u32[]{:S(2)}) collective-permute-start(f32[1,32,128]{2,1,0:T(8,128)S(1)} %get-tuple-element.47), channel_id=1, source_target_pairs={{32,0},{64,32},{96,64},{128,96},{160,128},{192,160},{224,192},{256... | collective-permute-start | bytes 49160 | tf_op jit(solution)/shard_map/ppermute | solution.py:20
  291.8 16.2 %collective-permute-start.24 = (f32[1,32,128]{2,1,0:T(8,128)S(1)}, f32[1,32,128]{2,1,0:T(8,128)S(1)}, u32[]{:S(2)}, u32[]{:S(2)}) collective-permute-start(f32[1,32,128]{2,1,0:T(8,128)S(1)} %get-tuple-element.46), channel_id=1, source_target_pairs={{0,32},{32,64},{64,96},{96,128},{128,160},{160,192},{192,224},{224... | collective-permute-start | bytes 49160 | tf_op jit(solution)/shard_map/ppermute | solution.py:19
  299.3 17.5 %all-to-all-start.9 = ((bf16[128,2,32]{2,1,0:T(2,128)(2,1)}), bf16[128,2,32]{2,1,0:T(2,128)(2,1)S(1)}, u32[]{:S(2)}, u32[]{:S(2)}) async-start(bf16[128,2,32]{2,1,0:T(2,128)(2,1)} %copy.466), calls=%async_computation.9 | async-start | bytes 131072 | tf_op jit(solution)/shard_map/all_to_all | solution.py:172
  308.0 15.2 %collective-permute-start.27 = (f32[18,1,128]{2,1,0:T(1,128)S(1)}, f32[18,1,128]{2,1,0:T(1,128)S(1)}, u32[]{:S(2)}, u32[]{:S(2)}) collective-permute-start(f32[18,1,128]{2,1,0:T(1,128)S(1)} %get-tuple-element.35), channel_id=1, source_target_pairs={{1,0},{2,1},{3,2},{4,3},{5,4},{6,5},{7,6},{9,8},{10,9},{11,10},{12... | collective-permute-start | bytes 27656 | tf_op jit(solution)/shard_map/ppermute | solution.py:20
  311.0 12.1 %collective-permute-start.26 = (f32[18,1,128]{2,1,0:T(1,128)S(1)}, f32[18,1,128]{2,1,0:T(1,128)S(1)}, u32[]{:S(2)}, u32[]{:S(2)}) collective-permute-start(f32[18,1,128]{2,1,0:T(1,128)S(1)} %get-tuple-element.34), channel_id=1, source_target_pairs={{0,1},{1,2},{2,3},{3,4},{4,5},{5,6},{6,7},{8,9},{9,10},{10,11},{11... | collective-permute-start | bytes 27656 | tf_op jit(solution)/shard_map/ppermute | solution.py:19
  318.8 10.0 %all-to-all-start.10 = ((bf16[8,2,512]{2,1,0:T(2,128)(2,1)}), bf16[8,2,512]{2,1,0:T(2,128)(2,1)S(1)}, u32[]{:S(2)}, u32[]{:S(2)}) async-start(bf16[8,2,512]{2,1,0:T(2,128)(2,1)} %reshape.226), calls=%async_computation.10 | async-start | bytes 32768 | tf_op jit(solution)/shard_map/all_to_all | solution.py:176
  331.8 11.4 %all-to-all-start.11 = ((bf16[4,2,1024]{2,1,0:T(2,128)(2,1)}), bf16[4,2,1024]{2,1,0:T(2,128)(2,1)S(1)}, u32[]{:S(2)}, u32[]{:S(2)}) async-start(bf16[4,2,1024]{2,1,0:T(2,128)(2,1)} %reshape.228), calls=%async_computation.11 | async-start | bytes 32768 | tf_op jit(solution)/shard_map/all_to_all | solution.py:178
  337.4 35.7 %collective-permute-start.29 = (f32[18,34,1]{2,1,0:T(8,128)}, f32[18,34,1]{2,1,0:T(8,128)}, u32[]{:S(2)}, u32[]{:S(2)}) collective-permute-start(f32[18,34,1]{2,1,0:T(8,128)} %get-tuple-element.23), channel_id=1, source_target_pairs={{8,0},{16,8},{24,16},{9,1},{17,9},{25,17},{10,2},{18,10},{26,18},{... | collective-permute-start | bytes 7352 | tf_op jit(solution)/shard_map/ppermute | solution.py:20
  339.3 33.8 %collective-permute-start.28 = (f32[18,34,1]{2,1,0:T(8,128)}, f32[18,34,1]{2,1,0:T(8,128)}, u32[]{:S(2)}, u32[]{:S(2)}) collective-permute-start(f32[18,34,1]{2,1,0:T(8,128)} %get-tuple-element.22), channel_id=1, source_target_pairs={{0,8},{8,16},{16,24},{1,9},{9,17},{17,25},{2,10},{10,18},{18,26},{... | collective-permute-start | bytes 7352 | tf_op jit(solution)/shard_map/ppermute | solution.py:19
  348.0 25.1 %copy-start.3 = (f32[16,32,128]{2,1,0:T(8,128)S(1)}, f32[16,32,128]{2,1,0:T(8,128)}, u32[]{:S(2)}) copy-start(f32[16,32,128]{2,1,0:T(8,128)} %copy-done.2) | copy-start | bytes 786436
  348.0 25.1 %copy-start.5 = (f32[16,32,128]{2,1,0:T(8,128)S(1)}, f32[16,32,128]{2,1,0:T(8,128)}, u32[]{:S(2)}) copy-start(f32[16,32,128]{2,1,0:T(8,128)} %get-tuple-element.18) | copy-start | bytes 786436
  364.3 8.9 %copy-start.9 = (f32[16,32,128]{2,1,0:T(8,128)S(1)}, f32[16,32,128]{2,1,0:T(8,128)}, u32[]{:S(2)}) copy-start(f32[16,32,128]{2,1,0:T(8,128)} %copy-done.8) | copy-start | bytes 786436
  364.3 42.1 %copy-start.7 = (f32[16,32,128]{2,1,0:T(8,128)S(1)}, f32[16,32,128]{2,1,0:T(8,128)}, u32[]{:S(2)}) copy-start(f32[16,32,128]{2,1,0:T(8,128)} %param.8) | copy-start | bytes 786436
  375.5 32.0 %copy-start = (f32[16,32,128]{2,1,0:T(8,128)}, f32[16,32,128]{2,1,0:T(8,128)S(1)}, u32[]{:S(2)}) copy-start(f32[16,32,128]{2,1,0:T(8,128)S(1)} %fusion.45) | copy-start | bytes 786436
  375.5 6.2 %collective-permute-start.31 = (f32[1,32,128]{2,1,0:T(8,128)S(1)}, f32[1,32,128]{2,1,0:T(8,128)S(1)}, u32[]{:S(2)}, u32[]{:S(2)}) collective-permute-start(f32[1,32,128]{2,1,0:T(8,128)S(1)} %get-tuple-element.45), channel_id=1, source_target_pairs={{32,0},{64,32},{96,64},{128,96},{160,128},{192,160},{224,192},{256... | collective-permute-start | bytes 49160 | tf_op jit(solution)/shard_map/ppermute | solution.py:20
  378.9 7.5 %collective-permute-start.30 = (f32[1,32,128]{2,1,0:T(8,128)S(1)}, f32[1,32,128]{2,1,0:T(8,128)S(1)}, u32[]{:S(2)}, u32[]{:S(2)}) collective-permute-start(f32[1,32,128]{2,1,0:T(8,128)S(1)} %get-tuple-element.44), channel_id=1, source_target_pairs={{0,32},{32,64},{64,96},{96,128},{128,160},{160,192},{192,224},{224... | collective-permute-start | bytes 49160 | tf_op jit(solution)/shard_map/ppermute | solution.py:19
  386.4 5.3 %collective-permute-start.33 = (f32[18,1,128]{2,1,0:T(1,128)S(1)}, f32[18,1,128]{2,1,0:T(1,128)S(1)}, u32[]{:S(2)}, u32[]{:S(2)}) collective-permute-start(f32[18,1,128]{2,1,0:T(1,128)S(1)} %get-tuple-element.33), channel_id=1, source_target_pairs={{1,0},{2,1},{3,2},{4,3},{5,4},{6,5},{7,6},{9,8},{10,9},{11,10},{12... | collective-permute-start | bytes 27656 | tf_op jit(solution)/shard_map/ppermute | solution.py:20
  389.4 4.4 %collective-permute-start.32 = (f32[18,1,128]{2,1,0:T(1,128)S(1)}, f32[18,1,128]{2,1,0:T(1,128)S(1)}, u32[]{:S(2)}, u32[]{:S(2)}) collective-permute-start(f32[18,1,128]{2,1,0:T(1,128)S(1)} %get-tuple-element.32), channel_id=1, source_target_pairs={{0,1},{1,2},{2,3},{3,4},{4,5},{5,6},{6,7},{8,9},{9,10},{10,11},{11... | collective-permute-start | bytes 27656 | tf_op jit(solution)/shard_map/ppermute | solution.py:19
  394.1 11.1 %collective-permute-start.35 = (f32[18,34,1]{2,1,0:T(8,128)S(1)}, f32[18,34,1]{2,1,0:T(8,128)S(1)}, u32[]{:S(2)}, u32[]{:S(2)}) collective-permute-start(f32[18,34,1]{2,1,0:T(8,128)S(1)} %get-tuple-element.21), channel_id=1, source_target_pairs={{8,0},{16,8},{24,16},{9,1},{17,9},{25,17},{10,2},{18,10},{26,18},{... | collective-permute-start | bytes 7352 | tf_op jit(solution)/shard_map/ppermute | solution.py:20
  398.4 8.0 %collective-permute-start.34 = (f32[18,34,1]{2,1,0:T(8,128)S(1)}, f32[18,34,1]{2,1,0:T(8,128)S(1)}, u32[]{:S(2)}, u32[]{:S(2)}) collective-permute-start(f32[18,34,1]{2,1,0:T(8,128)S(1)} %get-tuple-element.20), channel_id=1, source_target_pairs={{0,8},{8,16},{16,24},{1,9},{9,17},{17,25},{2,10},{10,18},{18,26},{... | collective-permute-start | bytes 7352 | tf_op jit(solution)/shard_map/ppermute | solution.py:19
  (2 other events, 1.2 us)
where the time goes:
time: 413 us; the launch traced here: 408 us
  starting transfers between devices  184 us (45%)
  local copies, waits for them, and re-layouts  76.9 us (19%)
  matrix products  57.7 us (14%)
  waiting for transfers between devices  53.9 us (13%)
  blocking collectives  17.6 us (4%)
  other arithmetic  13.9 us (3%)
    ppermute x18, starting transfers between devices, extended(): after = lax.ppermute(first, axis, down)  69.1 us
    ppermute x18, starting transfers between devices, extended(): before = lax.ppermute(last, axis, up)  50.9 us
    reshape x4, local copies, waits for them, and re-layouts, restrict_field(): blocks = field.reshape(count_x, 4, count_z, 4, count_y, 4)  31.9 us
    dot_general x2, matrix products, prolong_field(): jnp.einsum('kc,pizjyc->pizjyk', matrix, blocks, precision=lax.Precision.H...  31.7 us
    all_to_all x2, starting transfers between devices, coarse_correction(): lax.all_to_all(pencil, ('bx', 'by'), split_axis=0, concat_axis=1, tiled=T...  17.7 us
    all_to_all x2, starting transfers between devices, coarse_correction(): lax.all_to_all(pencil, ('bx', 'by'), split_axis=1, concat_axis=0, tiled=T...  17.2 us
    reshape x2, local copies, waits for them, and re-layouts, prolong_field(): return blocks.reshape(4 * count_x, 4 * count_z, 4 * count_y)  17 us
    ppermute x18, waiting for transfers between devices, extended(): before = lax.ppermute(last, axis, up)  17 us
  transfers between devices with their start and end apart: 46, of which 18 were waited for; matrix products, arithmetic and copies ran while one was open for 18% of the time, Pallas kernels for 0%

commit v1 on v0

--- a/solution.py
+++ b/solution.py
@@ -169,7 +169,10 @@
     pencil = jnp.einsum("ab,bzy->azy", table_x, pencil, preferred_element_type=jnp.float32).astype(
         jnp.bfloat16
     )
-    pencil = lax.all_to_all(pencil, ("bx", "by"), split_axis=0, concat_axis=1, tiled=True)
+    size = lax.axis_size(("bx", "by"))
+    shards = jnp.stack(jnp.split(pencil, size, axis=0), axis=0)
+    shards = lax.all_to_all(shards, ("bx", "by"), split_axis=0, concat_axis=0)
+    pencil = jnp.concatenate(shards, axis=1)
     pencil = jnp.einsum("ab,xbc->xac", table_z, pencil, preferred_element_type=jnp.float32).astype(
         jnp.bfloat16
     )

time: 413 us -> 518 us (1.25)
  local copies, waits for them, and re-layouts: 76.9 us -> 179 us
    unnamed x58 -> x184, local copies, waits for them, and re-layouts: 7.01 us -> 87.2 us
    split x0 -> x136, local copies, waits for them, and re-layouts: none -> 21.6 us  [coarse_correction(): shards = jnp.stack(jnp.split(pencil, size, axis=0), axis=0)]
  transfers between devices with their start and end apart: 46 -> 46, of which waited for: 18 -> 18; matrix products, arithmetic and copies ran while one was open for 18% -> 35% of each run, Pallas kernels for 0% -> 0%
where the time goes in v1:
time: 518 us; the launch traced here: 512 us
  starting transfers between devices  185 us (36%)
  local copies, waits for them, and re-layouts  179 us (35%)
  matrix products  58.6 us (11%)
  waiting for transfers between devices  53 us (10%)
  blocking collectives  17.6 us (3%)
  other arithmetic  13.8 us (3%)
    unnamed x184, local copies, waits for them, and re-layouts  87.2 us
    ppermute x18, starting transfers between devices, extended(): after = lax.ppermute(first, axis, down)  69 us
    ppermute x18, starting transfers between devices, extended(): before = lax.ppermute(last, axis, up)  51.2 us
    reshape x4, local copies, waits for them, and re-layouts, restrict_field(): blocks = field.reshape(count_x, 4, count_z, 4, count_y, 4)  31.9 us
    dot_general x2, matrix products, prolong_field(): jnp.einsum('kc,pizjyc->pizjyk', matrix, blocks, precision=lax.Precision.H...  31.8 us
    split x136, local copies, waits for them, and re-layouts, coarse_correction(): shards = jnp.stack(jnp.split(pencil, size, axis=0), axis=0)  21.6 us
    all_to_all x2, starting transfers between devices, coarse_correction(): shards = lax.all_to_all(shards, ('bx', 'by'), split_axis=0, concat_axis=0)  18.7 us
    all_to_all x2, starting transfers between devices, coarse_correction(): lax.all_to_all(pencil, ('bx', 'by'), split_axis=1, concat_axis=0, tiled=T...  17.2 us
  transfers between devices with their start and end apart: 46, of which 18 were waited for; matrix products, arithmetic and copies ran while one was open for 35% of the time, Pallas kernels for 0%

profile of v1, /device:TPU:11, one launch (start us, length us, event | category | flops | bytes accessed | tf_op | source)
XLA Modules:
  0.0 511.5 jit_solution(17565877623093549326)
XLA Ops:
  3.3 10.6 %collective-permute-start.1 = (f32[1,32,128]{2,1,0:T(8,128)S(1)}, f32[1,32,128]{2,1,0:T(8,128)S(1)}, u32[]{:S(2)}, u32[]{:S(2)}) collective-permute-start(f32[1,32,128]{2,1,0:T(8,128)S(1)} %copy.1046), channel_id=1, source_target_pairs={{32,0},{64,32},{96,64},{128,96},{160,128},{192,160},{224,192},{256... | collective-permute-start | bytes 49160 | tf_op jit(solution)/shard_map/ppermute | solution.py:20
  16.8 2.2 collective-permute-start.2
  19.0 6.1 %collective-permute-start.3 = (f32[1,32,128]{2,1,0:T(8,128)S(1)}, f32[1,32,128]{2,1,0:T(8,128)S(1)}, u32[]{:S(2)}, u32[]{:S(2)}) collective-permute-start(f32[1,32,128]{2,1,0:T(8,128)S(1)} %get-tuple-element.52), channel_id=1, source_target_pairs={{32,0},{64,32},{96,64},{128,96},{160,128},{192,160},{224,192},{256... | collective-permute-start | bytes 49160 | tf_op jit(solution)/shard_map/ppermute | solution.py:20
  28.7 2.1 collective-permute-start.5
  30.8 3.2 collective-permute-start.4
  34.1 2.1 collective-permute-start.7
  36.2 3.2 collective-permute-start.6
  39.8 4.5 collective-permute-start.9
  44.3 3.0 collective-permute-start.8
  49.5 3.8 collective-permute-start.10
  53.7 2.7 collective-permute-done.11
  58.8 10.1 %reshape.208 = f32[4,4,8,4,32,4]{5,4,3,2,1,0:T(8,128)} reshape(f32[16,32,128]{2,1,0:T(8,128)S(1)} %get-tuple-element.19) | data formatting | bytes 524288 | tf_op jit(solution)/shard_map/reshape | solution.py:100
  68.9 5.9 %copy.1054 = f32[4,4,8,4,32,4]{4,1,5,3,2,0:T(4,128)S(1)} copy(f32[4,4,8,4,32,4]{5,4,3,2,1,0:T(8,128)} %reshape.208) | data formatting | bytes 524288 | tf_op jit(solution)/shard_map/reshape | solution.py:100
  82.5 4.1 all-to-all-start
  86.6 3.1 all-to-all-done
  92.7 7.2 %all-to-all-start.1 = ((bf16[8,2,512]{2,1,0:T(2,128)(2,1)}), bf16[8,2,512]{2,1,0:T(2,128)(2,1)S(1)}, u32[]{:S(2)}, u32[]{:S(2)}) async-start(bf16[8,2,512]{2,1,0:T(2,128)(2,1)} %reshape.232), calls=%async_computation.1 | async-start | bytes 32768 | tf_op jit(solution)/shard_map/all_to_all | solution.py:143
  101.3 4.1 all-to-all-done.1
  106.9 9.5 %all-to-all-start.2 = ((bf16[2,128,32]{2,0,1:T(2,128)(2,1)}), bf16[2,128,32]{2,0,1:T(2,128)(2,1)S(1)}, u32[]{:S(2)}, u32[]{:S(2)}) async-start(bf16[2,128,32]{2,0,1:T(2,128)(2,1)} %copy.1062), calls=%async_computation.2 | async-start | bytes 131072 | tf_op jit(solution)/shard_map/all_to_all | solution.py:149
  117.0 5.2 %collective-permute-start.13 = (f32[1,32,128]{2,1,0:T(8,128)}, f32[1,32,128]{2,1,0:T(8,128)S(1)}, u32[]{:S(2)}, u32[]{:S(2)}) collective-permute-start(f32[1,32,128]{2,1,0:T(8,128)} %get-tuple-element.51), channel_id=1, source_target_pairs={{32,0},{64,32},{96,64},{128,96},{160,128},{192,160},{224,192},{256... | collective-permute-start | bytes 49160 | tf_op jit(solution)/shard_map/ppermute | solution.py:20
  122.2 2.1 collective-permute-start.12
  177.5 9.4 %all-to-all-start.3 = ((bf16[64,2,2,32]{3,2,1,0:T(2,128)(2,1)}), bf16[64,2,2,32]{3,2,1,0:T(2,128)(2,1)S(1)}, u32[]{:S(2)}, u32[]{:S(2)}) async-start(bf16[64,2,2,32]{3,2,1,0:T(2,128)(2,1)} %constant_dynamic-update-slice_fusion.3), calls=%async_computation.3 | async-start | bytes 131072 | tf_op jit(solution)/shard_map/all_to_all | solution.py:174
  187.0 3.0 collective-permute-start.15
  190.0 2.2 collective-permute-start.14
  192.2 3.5 all-to-all-done.3
  197.7 4.4 all-to-all-start.4
  202.2 5.6 %all-to-all-done.4 = bf16[8,2,512]{2,1,0:T(2,128)(2,1)S(1)} async-done(((bf16[8,2,512]{2,1,0:T(2,128)(2,1)}), bf16[8,2,512]{2,1,0:T(2,128)(2,1)S(1)}, u32[]{:S(2)}, u32[]{:S(2)}) %all-to-all-start.4) | async-done | bytes 16416 | tf_op jit(solution)/shard_map/all_to_all | solution.py:179
  210.8 4.6 all-to-all-start.5
  218.3 4.1 collective-permute-start.16
  225.9 15.5 %fusion.9 = f32[4,4,8,4,32,4]{5,4,3,2,1,0:T(8,128)} fusion(f32[4,2,1,1,1,1]{0,1,5,4,3,2:T(2,128)S(1)} %copy-done.13, f32[4,4,8,4,32,2]{4,3,5,2,1,0:T(4,128)S(1)} %convolution_bitcast_fusion.2), kind=kOutput, calls=%fused_computation.37 | convolution fusion | flops 1572864 | bytes 393248 | tf_op jit(solution)/shard_map/kc,pizjyc->pizjyk/dot_general | solution.py:114
  241.4 8.2 %reshape.212 = f32[16,32,128]{2,1,0:T(8,128)S(1)} reshape(f32[4,4,8,4,32,4]{5,4,3,2,1,0:T(8,128)} %fusion.9) | data formatting | bytes 524288 | tf_op jit(solution)/shard_map/reshape | solution.py:115
  251.3 3.3 collective-permute-start.19
  254.6 2.8 collective-permute-start.18
  257.5 4.6 collective-permute-done.18
  262.1 3.0 collective-permute-start.21
  265.2 2.4 collective-permute-start.20
  269.8 4.3 collective-permute-start.23
  274.1 3.5 collective-permute-start.22
  277.6 3.3 collective-permute-done.23
  284.2 10.1 %reshape.213 = f32[4,4,8,4,32,4]{5,4,3,2,1,0:T(8,128)} reshape(f32[16,32,128]{2,1,0:T(8,128)S(1)} %get-tuple-element.16) | data formatting | bytes 524288 | tf_op jit(solution)/shard_map/reshape | solution.py:100
  294.3 5.9 %copy.1144 = f32[4,4,8,4,32,4]{4,1,5,3,2,0:T(4,128)S(1)} copy(f32[4,4,8,4,32,4]{5,4,3,2,1,0:T(8,128)} %reshape.213) | data formatting | bytes 524288 | tf_op jit(solution)/shard_map/reshape | solution.py:100
  308.1 7.1 %all_to_all.184 = bf16[4,2,1024]{2,1,0:T(2,128)(2,1)S(1)} all-to-all(bf16[4,2,1024]{2,1,0:T(2,128)(2,1)S(1)} %reshape.238), channel_id=1, replica_groups=mesh['bx'=16,'by'=4,'bz'=8] {'by'}, dimensions={0} | all-to-all | bytes 32768 | tf_op jit(solution)/shard_map/all_to_all | solution.py:139
  317.5 10.5 %all_to_all.185 = bf16[8,2,512]{2,1,0:T(2,128)(2,1)S(1)} all-to-all(bf16[8,2,512]{2,1,0:T(2,128)(2,1)S(1)} %reshape.240), channel_id=1, replica_groups=mesh['bx'=16,'by'=4,'bz'=8] {'bz'}, dimensions={0} | all-to-all | bytes 32768 | tf_op jit(solution)/shard_map/all_to_all | solution.py:143
  330.2 7.7 %all-to-all-start.8 = ((bf16[2,128,32]{2,0,1:T(2,128)(2,1)}), bf16[2,128,32]{2,0,1:T(2,128)(2,1)S(1)}, u32[]{:S(2)}, u32[]{:S(2)}) async-start(bf16[2,128,32]{2,0,1:T(2,128)(2,1)} %copy.1152), calls=%async_computation.8 | async-start | bytes 131072 | tf_op jit(solution)/shard_map/all_to_all | solution.py:149
  338.5 5.2 %collective-permute-start.25 = (f32[1,32,128]{2,1,0:T(8,128)}, f32[1,32,128]{2,1,0:T(8,128)S(1)}, u32[]{:S(2)}, u32[]{:S(2)}) collective-permute-start(f32[1,32,128]{2,1,0:T(8,128)} %get-tuple-element.47), channel_id=1, source_target_pairs={{32,0},{64,32},{96,64},{128,96},{160,128},{192,160},{224,192},{256... | collective-permute-start | bytes 49160 | tf_op jit(solution)/shard_map/ppermute | solution.py:20
  402.5 9.2 %all-to-all-start.9 = ((bf16[64,2,2,32]{3,2,1,0:T(2,128)(2,1)}), bf16[64,2,2,32]{3,2,1,0:T(2,128)(2,1)S(1)}, u32[]{:S(2)}, u32[]{:S(2)}) async-start(bf16[64,2,2,32]{3,2,1,0:T(2,128)(2,1)} %constant_dynamic-update-slice_fusion.67), calls=%async_computation.9 | async-start | bytes 131072 | tf_op jit(solution)/shard_map/all_to_all | solution.py:174
  411.8 3.0 collective-permute-start.27
  414.8 2.2 collective-permute-start.26
  417.1 3.5 all-to-all-done.9
  422.6 4.4 all-to-all-start.10
  427.6 5.0 all-to-all-done.10
  435.6 4.6 all-to-all-start.11
  443.1 3.8 collective-permute-start.28
  451.8 16.3 %fusion.6 = f32[4,4,8,4,32,4]{5,4,3,2,1,0:T(8,128)} fusion(f32[4,2,1,1,1,1]{0,1,5,4,3,2:T(2,128)} %constant.103, f32[4,4,8,4,32,2]{4,3,5,2,1,0:T(4,128)S(1)} %convolution_bitcast_fusion), kind=kOutput, calls=%fused_computation.34 | convolution fusion | flops 1572864 | bytes 393248 | tf_op jit(solution)/shard_map/kc,pizjyc->pizjyk/dot_general | solution.py:114
  468.1 8.8 %reshape.217 = f32[16,32,128]{2,1,0:T(8,128)} reshape(f32[4,4,8,4,32,4]{5,4,3,2,1,0:T(8,128)} %fusion.6) | data formatting | bytes 524288 | tf_op jit(solution)/shard_map/reshape | solution.py:115
  477.0 2.3 fusion.45
  479.3 3.3 collective-permute-start.31
  482.7 2.8 collective-permute-start.30
  485.5 4.6 collective-permute-done.30
  490.2 3.0 collective-permute-start.33
  493.2 2.2 collective-permute-start.32
  495.5 2.1 collective-permute-done.32
  497.9 4.3 collective-permute-start.35
  502.2 3.5 collective-permute-start.34
  505.7 3.3 collective-permute-done.35
  (492 shorter events, 186.0 us)
Async XLA Ops:
  0.6 33.4 %copy-start.1 = (f32[16,32,128]{2,1,0:T(8,128)S(1)}, f32[16,32,128]{2,1,0:T(8,128)}, u32[]{:S(2)}) copy-start(f32[16,32,128]{2,1,0:T(8,128)} %param.9) | copy-start | bytes 786436
  3.3 25.4 %collective-permute-start.1 = (f32[1,32,128]{2,1,0:T(8,128)S(1)}, f32[1,32,128]{2,1,0:T(8,128)S(1)}, u32[]{:S(2)}, u32[]{:S(2)}) collective-permute-start(f32[1,32,128]{2,1,0:T(8,128)S(1)} %copy.1046), channel_id=1, source_target_pairs={{32,0},{64,32},{96,64},{128,96},{160,128},{192,160},{224,192},{256... | collective-permute-start | bytes 49160 | tf_op jit(solution)/shard_map/ppermute | solution.py:20
  14.1 14.6 %collective-permute-start = (f32[1,32,128]{2,1,0:T(8,128)S(1)}, f32[1,32,128]{2,1,0:T(8,128)S(1)}, u32[]{:S(2)}, u32[]{:S(2)}) collective-permute-start(f32[1,32,128]{2,1,0:T(8,128)S(1)} %copy.1042), channel_id=1, source_target_pairs={{0,32},{32,64},{64,96},{96,128},{128,160},{160,192},{192,224},{224... | collective-permute-start | bytes 49160 | tf_op jit(solution)/shard_map/ppermute | solution.py:19
  16.8 17.3 %collective-permute-start.2 = (f32[1,32,128]{2,1,0:T(8,128)S(1)}, f32[1,32,128]{2,1,0:T(8,128)S(1)}, u32[]{:S(2)}, u32[]{:S(2)}) collective-permute-start(f32[1,32,128]{2,1,0:T(8,128)S(1)} %get-tuple-element.53), channel_id=1, source_target_pairs={{0,32},{32,64},{64,96},{96,128},{128,160},{160,192},{192,224},{224... | collective-permute-start | bytes 49160 | tf_op jit(solution)/shard_map/ppermute | solution.py:19
  19.0 15.1 %collective-permute-start.3 = (f32[1,32,128]{2,1,0:T(8,128)S(1)}, f32[1,32,128]{2,1,0:T(8,128)S(1)}, u32[]{:S(2)}, u32[]{:S(2)}) collective-permute-start(f32[1,32,128]{2,1,0:T(8,128)S(1)} %get-tuple-element.52), channel_id=1, source_target_pairs={{32,0},{64,32},{96,64},{128,96},{160,128},{192,160},{224,192},{256... | collective-permute-start | bytes 49160 | tf_op jit(solution)/shard_map/ppermute | solution.py:20
  26.8 30.8 %copy-start.6 = (f32[16,32,128]{2,1,0:T(8,128)S(1)}, f32[16,32,128]{2,1,0:T(8,128)}, u32[]{:S(2)}) copy-start(f32[16,32,128]{2,1,0:T(8,128)} %param.8) | copy-start | bytes 786436
  28.7 10.8 %collective-permute-start.5 = (f32[18,1,128]{2,1,0:T(1,128)S(1)}, f32[18,1,128]{2,1,0:T(1,128)S(1)}, u32[]{:S(2)}, u32[]{:S(2)}) collective-permute-start(f32[18,1,128]{2,1,0:T(1,128)S(1)} %get-tuple-element.43), channel_id=1, source_target_pairs={{1,0},{2,1},{3,2},{4,3},{5,4},{6,5},{7,6},{9,8},{10,9},{11,10},{12... | collective-permute-start | bytes 27656 | tf_op jit(solution)/shard_map/ppermute | solution.py:20
  30.8 8.7 %collective-permute-start.4 = (f32[18,1,128]{2,1,0:T(1,128)S(1)}, f32[18,1,128]{2,1,0:T(1,128)S(1)}, u32[]{:S(2)}, u32[]{:S(2)}) collective-permute-start(f32[18,1,128]{2,1,0:T(1,128)S(1)} %get-tuple-element.42), channel_id=1, source_target_pairs={{0,1},{1,2},{2,3},{3,4},{4,5},{5,6},{6,7},{8,9},{9,10},{10,11},{11... | collective-permute-start | bytes 27656 | tf_op jit(solution)/shard_map/ppermute | solution.py:19
  34.1 13.2 %collective-permute-start.7 = (f32[18,1,128]{2,1,0:T(1,128)S(1)}, f32[18,1,128]{2,1,0:T(1,128)S(1)}, u32[]{:S(2)}, u32[]{:S(2)}) collective-permute-start(f32[18,1,128]{2,1,0:T(1,128)S(1)} %get-tuple-element.41), channel_id=1, source_target_pairs={{1,0},{2,1},{3,2},{4,3},{5,4},{6,5},{7,6},{9,8},{10,9},{11,10},{12... | collective-permute-start | bytes 27656 | tf_op jit(solution)/shard_map/ppermute | solution.py:20
  36.2 11.1 %collective-permute-start.6 = (f32[18,1,128]{2,1,0:T(1,128)S(1)}, f32[18,1,128]{2,1,0:T(1,128)S(1)}, u32[]{:S(2)}, u32[]{:S(2)}) collective-permute-start(f32[18,1,128]{2,1,0:T(1,128)S(1)} %get-tuple-element.40), channel_id=1, source_target_pairs={{0,1},{1,2},{2,3},{3,4},{4,5},{5,6},{6,7},{8,9},{9,10},{10,11},{11... | collective-permute-start | bytes 27656 | tf_op jit(solution)/shard_map/ppermute | solution.py:19
  39.8 13.7 %collective-permute-start.9 = (f32[18,34,1]{2,1,0:T(8,128)S(1)}, f32[18,34,1]{2,1,0:T(8,128)S(1)}, u32[]{:S(2)}, u32[]{:S(2)}) collective-permute-start(f32[18,34,1]{2,1,0:T(8,128)S(1)} %get-tuple-element.31), channel_id=1, source_target_pairs={{8,0},{16,8},{24,16},{9,1},{17,9},{25,17},{10,2},{18,10},{26,18},{... | collective-permute-start | bytes 7352 | tf_op jit(solution)/shard_map/ppermute | solution.py:20
  44.3 9.1 %collective-permute-start.8 = (f32[18,34,1]{2,1,0:T(8,128)S(1)}, f32[18,34,1]{2,1,0:T(8,128)S(1)}, u32[]{:S(2)}, u32[]{:S(2)}) collective-permute-start(f32[18,34,1]{2,1,0:T(8,128)S(1)} %get-tuple-element.30), channel_id=1, source_target_pairs={{0,8},{8,16},{16,24},{1,9},{9,17},{17,25},{2,10},{10,18},{18,26},{... | collective-permute-start | bytes 7352 | tf_op jit(solution)/shard_map/ppermute | solution.py:19
  47.6 8.8 %collective-permute-start.11 = (f32[18,34,1]{2,1,0:T(8,128)S(1)}, f32[18,34,1]{2,1,0:T(8,128)S(1)}, u32[]{:S(2)}, u32[]{:S(2)}) collective-permute-start(f32[18,34,1]{2,1,0:T(8,128)S(1)} %get-tuple-element.29), channel_id=1, source_target_pairs={{8,0},{16,8},{24,16},{9,1},{17,9},{25,17},{10,2},{18,10},{26,18},{... | collective-permute-start | bytes 7352 | tf_op jit(solution)/shard_map/ppermute | solution.py:20
  49.5 8.1 %collective-permute-start.10 = (f32[18,34,1]{2,1,0:T(8,128)S(1)}, f32[18,34,1]{2,1,0:T(8,128)S(1)}, u32[]{:S(2)}, u32[]{:S(2)}) collective-permute-start(f32[18,34,1]{2,1,0:T(8,128)S(1)} %get-tuple-element.28), channel_id=1, source_target_pairs={{0,8},{8,16},{16,24},{1,9},{9,17},{17,25},{2,10},{10,18},{18,26},{... | collective-permute-start | bytes 7352 | tf_op jit(solution)/shard_map/ppermute | solution.py:19
  58.8 190.9 %copy-start.2 = (f32[16,32,128]{2,1,0:T(8,128)}, f32[16,32,128]{2,1,0:T(8,128)S(1)}, u32[]{:S(2)}) copy-start(f32[16,32,128]{2,1,0:T(8,128)S(1)} %get-tuple-element.19) | copy-start | bytes 786436
  58.8 16.0 %copy-start.16 = (f32[2,4,1,1,1,1]{1,0,5,4,3,2:T(2,128)S(1)}, f32[2,4,1,1,1,1]{1,0,5,4,3,2:T(2,128)}, u32[]{:S(2)}) copy-start(f32[2,4,1,1,1,1]{1,0,5,4,3,2:T(2,128)} %constant.102) | copy-start | bytes 100
  79.8 144.6 %copy-start.13 = (f32[4,2,1,1,1,1]{0,1,5,4,3,2:T(2,128)S(1)}, f32[4,2,1,1,1,1]{0,1,5,4,3,2:T(2,128)}, u32[]{:S(2)}) copy-start(f32[4,2,1,1,1,1]{0,1,5,4,3,2:T(2,128)} %constant.103) | copy-start | bytes 100
  82.5 7.3 %all-to-all-start = ((bf16[4,2,1024]{2,1,0:T(2,128)(2,1)}), bf16[4,2,1024]{2,1,0:T(2,128)(2,1)S(1)}, u32[]{:S(2)}, u32[]{:S(2)}) async-start(bf16[4,2,1024]{2,1,0:T(2,128)(2,1)} %reshape.230), calls=%async_computation | async-start | bytes 32768 | tf_op jit(solution)/shard_map/all_to_all | solution.py:139
  86.6 50.7 %copy-start.19 = (s32[128]{0:T(128)}, s32[128]{0:T(128)S(1)}, u32[]{:S(2)}) copy-start(s32[128]{0:T(128)S(1)} %iota_add_fusion.1) | copy-start | bytes 1540
  92.7 12.7 %all-to-all-start.1 = ((bf16[8,2,512]{2,1,0:T(2,128)(2,1)}), bf16[8,2,512]{2,1,0:T(2,128)(2,1)S(1)}, u32[]{:S(2)}, u32[]{:S(2)}) async-start(bf16[8,2,512]{2,1,0:T(2,128)(2,1)} %reshape.232), calls=%async_computation.1 | async-start | bytes 32768 | tf_op jit(solution)/shard_map/all_to_all | solution.py:143
  100.0 37.5 %copy-start.18 = (f32[32]{0:T(128)}, f32[32]{0:T(128)S(1)}, u32[]{:S(2)}) copy-start(f32[32]{0:T(128)S(1)} %multiply_subtract_fusion) | copy-start | bytes 388
  106.9 18.4 %all-to-all-start.2 = ((bf16[2,128,32]{2,0,1:T(2,128)(2,1)}), bf16[2,128,32]{2,0,1:T(2,128)(2,1)S(1)}, u32[]{:S(2)}, u32[]{:S(2)}) async-start(bf16[2,128,32]{2,0,1:T(2,128)(2,1)} %copy.1062), calls=%async_computation.2 | async-start | bytes 131072 | tf_op jit(solution)/shard_map/all_to_all | solution.py:149
  117.0 69.9 %collective-permute-start.13 = (f32[1,32,128]{2,1,0:T(8,128)}, f32[1,32,128]{2,1,0:T(8,128)S(1)}, u32[]{:S(2)}, u32[]{:S(2)}) collective-permute-start(f32[1,32,128]{2,1,0:T(8,128)} %get-tuple-element.51), channel_id=1, source_target_pairs={{32,0},{64,32},{96,64},{128,96},{160,128},{192,160},{224,192},{256... | collective-permute-start | bytes 49160 | tf_op jit(solution)/shard_map/ppermute | solution.py:20
  122.2 64.7 %collective-permute-start.12 = (f32[1,32,128]{2,1,0:T(8,128)}, f32[1,32,128]{2,1,0:T(8,128)S(1)}, u32[]{:S(2)}, u32[]{:S(2)}) collective-permute-start(f32[1,32,128]{2,1,0:T(8,128)} %get-tuple-element.50), channel_id=1, source_target_pairs={{0,32},{32,64},{64,96},{96,128},{128,160},{160,192},{192,224},{224... | collective-permute-start | bytes 49160 | tf_op jit(solution)/shard_map/ppermute | solution.py:19
  177.5 18.3 %all-to-all-start.3 = ((bf16[64,2,2,32]{3,2,1,0:T(2,128)(2,1)}), bf16[64,2,2,32]{3,2,1,0:T(2,128)(2,1)S(1)}, u32[]{:S(2)}, u32[]{:S(2)}) async-start(bf16[64,2,2,32]{3,2,1,0:T(2,128)(2,1)} %constant_dynamic-update-slice_fusion.3), calls=%async_computation.3 | async-start | bytes 131072 | tf_op jit(solution)/shard_map/all_to_all | solution.py:174
  187.0 15.2 %collective-permute-start.15 = (f32[18,1,128]{2,1,0:T(1,128)S(1)}, f32[18,1,128]{2,1,0:T(1,128)S(1)}, u32[]{:S(2)}, u32[]{:S(2)}) collective-permute-start(f32[18,1,128]{2,1,0:T(1,128)S(1)} %get-tuple-element.39), channel_id=1, source_target_pairs={{1,0},{2,1},{3,2},{4,3},{5,4},{6,5},{7,6},{9,8},{10,9},{11,10},{12... | collective-permute-start | bytes 27656 | tf_op jit(solution)/shard_map/ppermute | solution.py:20
  190.0 12.1 %collective-permute-start.14 = (f32[18,1,128]{2,1,0:T(1,128)S(1)}, f32[18,1,128]{2,1,0:T(1,128)S(1)}, u32[]{:S(2)}, u32[]{:S(2)}) collective-permute-start(f32[18,1,128]{2,1,0:T(1,128)S(1)} %get-tuple-element.38), channel_id=1, source_target_pairs={{0,1},{1,2},{2,3},{3,4},{4,5},{5,6},{6,7},{8,9},{9,10},{10,11},{11... | collective-permute-start | bytes 27656 | tf_op jit(solution)/shard_map/ppermute | solution.py:19
  197.7 10.0 %all-to-all-start.4 = ((bf16[8,2,512]{2,1,0:T(2,128)(2,1)}), bf16[8,2,512]{2,1,0:T(2,128)(2,1)S(1)}, u32[]{:S(2)}, u32[]{:S(2)}) async-start(bf16[8,2,512]{2,1,0:T(2,128)(2,1)} %reshape.234), calls=%async_computation.4 | async-start | bytes 32768 | tf_op jit(solution)/shard_map/all_to_all | solution.py:179
  202.1 47.5 %copy-start.11 = (f32[18,1,128]{2,1,0:T(1,128)}, f32[18,1,128]{2,1,0:T(1,128)S(1)}, u32[]{:S(2)}) copy-start(f32[18,1,128]{2,1,0:T(1,128)S(1)} %collective-permute-done.15) | copy-start | bytes 27652
  202.1 47.5 %copy-start.12 = (f32[18,1,128]{2,1,0:T(1,128)}, f32[18,1,128]{2,1,0:T(1,128)S(1)}, u32[]{:S(2)}) copy-start(f32[18,1,128]{2,1,0:T(1,128)S(1)} %collective-permute-done.14) | copy-start | bytes 27652
  210.8 11.6 %all-to-all-start.5 = ((bf16[4,2,1024]{2,1,0:T(2,128)(2,1)}), bf16[4,2,1024]{2,1,0:T(2,128)(2,1)S(1)}, u32[]{:S(2)}, u32[]{:S(2)}) async-start(bf16[4,2,1024]{2,1,0:T(2,128)(2,1)} %reshape.236), calls=%async_computation.5 | async-start | bytes 32768 | tf_op jit(solution)/shard_map/all_to_all | solution.py:181
  216.4 33.2 %collective-permute-start.17 = (f32[18,34,1]{2,1,0:T(8,128)}, f32[18,34,1]{2,1,0:T(8,128)}, u32[]{:S(2)}, u32[]{:S(2)}) collective-permute-start(f32[18,34,1]{2,1,0:T(8,128)} %get-tuple-element.27), channel_id=1, source_target_pairs={{8,0},{16,8},{24,16},{9,1},{17,9},{25,17},{10,2},{18,10},{26,18},{... | collective-permute-start | bytes 7352 | tf_op jit(solution)/shard_map/ppermute | solution.py:20
  218.3 31.3 %collective-permute-start.16 = (f32[18,34,1]{2,1,0:T(8,128)}, f32[18,34,1]{2,1,0:T(8,128)}, u32[]{:S(2)}, u32[]{:S(2)}) collective-permute-start(f32[18,34,1]{2,1,0:T(8,128)} %get-tuple-element.26), channel_id=1, source_target_pairs={{0,8},{8,16},{16,24},{1,9},{9,17},{17,25},{2,10},{10,18},{18,26},{... | collective-permute-start | bytes 7352 | tf_op jit(solution)/shard_map/ppermute | solution.py:19
  225.9 23.8 %copy-start.4 = (f32[16,32,128]{2,1,0:T(8,128)S(1)}, f32[16,32,128]{2,1,0:T(8,128)}, u32[]{:S(2)}) copy-start(f32[16,32,128]{2,1,0:T(8,128)} %get-tuple-element.18) | copy-start | bytes 786436
  249.6 31.3 %copy-start.8 = (f32[16,32,128]{2,1,0:T(8,128)}, f32[16,32,128]{2,1,0:T(8,128)S(1)}, u32[]{:S(2)}) copy-start(f32[16,32,128]{2,1,0:T(8,128)S(1)} %reshape.212) | copy-start | bytes 786436
  251.3 6.2 %collective-permute-start.19 = (f32[1,32,128]{2,1,0:T(8,128)S(1)}, f32[1,32,128]{2,1,0:T(8,128)S(1)}, u32[]{:S(2)}, u32[]{:S(2)}) collective-permute-start(f32[1,32,128]{2,1,0:T(8,128)S(1)} %get-tuple-element.49), channel_id=1, source_target_pairs={{32,0},{64,32},{96,64},{128,96},{160,128},{192,160},{224,192},{256... | collective-permute-start | bytes 49160 | tf_op jit(solution)/shard_map/ppermute | solution.py:20
  254.6 7.5 %collective-permute-start.18 = (f32[1,32,128]{2,1,0:T(8,128)S(1)}, f32[1,32,128]{2,1,0:T(8,128)S(1)}, u32[]{:S(2)}, u32[]{:S(2)}) collective-permute-start(f32[1,32,128]{2,1,0:T(8,128)S(1)} %get-tuple-element.48), channel_id=1, source_target_pairs={{0,32},{32,64},{64,96},{96,128},{128,160},{160,192},{192,224},{224... | collective-permute-start | bytes 49160 | tf_op jit(solution)/shard_map/ppermute | solution.py:19
  262.1 5.5 %collective-permute-start.21 = (f32[18,1,128]{2,1,0:T(1,128)S(1)}, f32[18,1,128]{2,1,0:T(1,128)S(1)}, u32[]{:S(2)}, u32[]{:S(2)}) collective-permute-start(f32[18,1,128]{2,1,0:T(1,128)S(1)} %get-tuple-element.37), channel_id=1, source_target_pairs={{1,0},{2,1},{3,2},{4,3},{5,4},{6,5},{7,6},{9,8},{10,9},{11,10},{12... | collective-permute-start | bytes 27656 | tf_op jit(solution)/shard_map/ppermute | solution.py:20
  265.2 4.4 collective-permute-start.20
  269.8 11.1 %collective-permute-start.23 = (f32[18,34,1]{2,1,0:T(8,128)S(1)}, f32[18,34,1]{2,1,0:T(8,128)S(1)}, u32[]{:S(2)}, u32[]{:S(2)}) collective-permute-start(f32[18,34,1]{2,1,0:T(8,128)S(1)} %get-tuple-element.25), channel_id=1, source_target_pairs={{8,0},{16,8},{24,16},{9,1},{17,9},{25,17},{10,2},{18,10},{26,18},{... | collective-permute-start | bytes 7352 | tf_op jit(solution)/shard_map/ppermute | solution.py:20
  274.1 8.0 %collective-permute-start.22 = (f32[18,34,1]{2,1,0:T(8,128)S(1)}, f32[18,34,1]{2,1,0:T(8,128)S(1)}, u32[]{:S(2)}, u32[]{:S(2)}) collective-permute-start(f32[18,34,1]{2,1,0:T(8,128)S(1)} %get-tuple-element.24), channel_id=1, source_target_pairs={{0,8},{8,16},{16,24},{1,9},{9,17},{17,25},{2,10},{10,18},{18,26},{... | collective-permute-start | bytes 7352 | tf_op jit(solution)/shard_map/ppermute | solution.py:19
  283.5 0.7 copy-start.10
  284.2 16.0 %copy-start.17 = (f32[2,4,1,1,1,1]{1,0,5,4,3,2:T(2,128)S(1)}, f32[2,4,1,1,1,1]{1,0,5,4,3,2:T(2,128)}, u32[]{:S(2)}) copy-start(f32[2,4,1,1,1,1]{1,0,5,4,3,2:T(2,128)} %constant.102) | copy-start | bytes 100
  330.2 16.5 %all-to-all-start.8 = ((bf16[2,128,32]{2,0,1:T(2,128)(2,1)}), bf16[2,128,32]{2,0,1:T(2,128)(2,1)S(1)}, u32[]{:S(2)}, u32[]{:S(2)}) async-start(bf16[2,128,32]{2,0,1:T(2,128)(2,1)} %copy.1152), calls=%async_computation.8 | async-start | bytes 131072 | tf_op jit(solution)/shard_map/all_to_all | solution.py:149
  338.5 73.2 %collective-permute-start.25 = (f32[1,32,128]{2,1,0:T(8,128)}, f32[1,32,128]{2,1,0:T(8,128)S(1)}, u32[]{:S(2)}, u32[]{:S(2)}) collective-permute-start(f32[1,32,128]{2,1,0:T(8,128)} %get-tuple-element.47), channel_id=1, source_target_pairs={{32,0},{64,32},{96,64},{128,96},{160,128},{192,160},{224,192},{256... | collective-permute-start | bytes 49160 | tf_op jit(solution)/shard_map/ppermute | solution.py:20
  343.7 68.0 %collective-permute-start.24 = (f32[1,32,128]{2,1,0:T(8,128)}, f32[1,32,128]{2,1,0:T(8,128)S(1)}, u32[]{:S(2)}, u32[]{:S(2)}) collective-permute-start(f32[1,32,128]{2,1,0:T(8,128)} %get-tuple-element.46), channel_id=1, source_target_pairs={{0,32},{32,64},{64,96},{96,128},{128,160},{160,192},{192,224},{224... | collective-permute-start | bytes 49160 | tf_op jit(solution)/shard_map/ppermute | solution.py:19
  402.5 18.0 %all-to-all-start.9 = ((bf16[64,2,2,32]{3,2,1,0:T(2,128)(2,1)}), bf16[64,2,2,32]{3,2,1,0:T(2,128)(2,1)S(1)}, u32[]{:S(2)}, u32[]{:S(2)}) async-start(bf16[64,2,2,32]{3,2,1,0:T(2,128)(2,1)} %constant_dynamic-update-slice_fusion.67), calls=%async_computation.9 | async-start | bytes 131072 | tf_op jit(solution)/shard_map/all_to_all | solution.py:174
  411.8 15.2 %collective-permute-start.27 = (f32[18,1,128]{2,1,0:T(1,128)S(1)}, f32[18,1,128]{2,1,0:T(1,128)S(1)}, u32[]{:S(2)}, u32[]{:S(2)}) collective-permute-start(f32[18,1,128]{2,1,0:T(1,128)S(1)} %get-tuple-element.35), channel_id=1, source_target_pairs={{1,0},{2,1},{3,2},{4,3},{5,4},{6,5},{7,6},{9,8},{10,9},{11,10},{12... | collective-permute-start | bytes 27656 | tf_op jit(solution)/shard_map/ppermute | solution.py:20
  414.8 12.1 %collective-permute-start.26 = (f32[18,1,128]{2,1,0:T(1,128)S(1)}, f32[18,1,128]{2,1,0:T(1,128)S(1)}, u32[]{:S(2)}, u32[]{:S(2)}) collective-permute-start(f32[18,1,128]{2,1,0:T(1,128)S(1)} %get-tuple-element.34), channel_id=1, source_target_pairs={{0,1},{1,2},{2,3},{3,4},{4,5},{5,6},{6,7},{8,9},{9,10},{10,11},{11... | collective-permute-start | bytes 27656 | tf_op jit(solution)/shard_map/ppermute | solution.py:19
  422.6 10.0 %all-to-all-start.10 = ((bf16[8,2,512]{2,1,0:T(2,128)(2,1)}), bf16[8,2,512]{2,1,0:T(2,128)(2,1)S(1)}, u32[]{:S(2)}, u32[]{:S(2)}) async-start(bf16[8,2,512]{2,1,0:T(2,128)(2,1)} %reshape.242), calls=%async_computation.10 | async-start | bytes 32768 | tf_op jit(solution)/shard_map/all_to_all | solution.py:179
  435.6 11.4 %all-to-all-start.11 = ((bf16[4,2,1024]{2,1,0:T(2,128)(2,1)}), bf16[4,2,1024]{2,1,0:T(2,128)(2,1)S(1)}, u32[]{:S(2)}, u32[]{:S(2)}) async-start(bf16[4,2,1024]{2,1,0:T(2,128)(2,1)} %reshape.244), calls=%async_computation.11 | async-start | bytes 32768 | tf_op jit(solution)/shard_map/all_to_all | solution.py:181
  441.2 35.7 %collective-permute-start.29 = (f32[18,34,1]{2,1,0:T(8,128)}, f32[18,34,1]{2,1,0:T(8,128)}, u32[]{:S(2)}, u32[]{:S(2)}) collective-permute-start(f32[18,34,1]{2,1,0:T(8,128)} %get-tuple-element.23), channel_id=1, source_target_pairs={{8,0},{16,8},{24,16},{9,1},{17,9},{25,17},{10,2},{18,10},{26,18},{... | collective-permute-start | bytes 7352 | tf_op jit(solution)/shard_map/ppermute | solution.py:20
  443.1 33.8 %collective-permute-start.28 = (f32[18,34,1]{2,1,0:T(8,128)}, f32[18,34,1]{2,1,0:T(8,128)}, u32[]{:S(2)}, u32[]{:S(2)}) collective-permute-start(f32[18,34,1]{2,1,0:T(8,128)} %get-tuple-element.22), channel_id=1, source_target_pairs={{0,8},{8,16},{16,24},{1,9},{9,17},{17,25},{2,10},{10,18},{18,26},{... | collective-permute-start | bytes 7352 | tf_op jit(solution)/shard_map/ppermute | solution.py:19
  451.8 25.1 %copy-start.3 = (f32[16,32,128]{2,1,0:T(8,128)S(1)}, f32[16,32,128]{2,1,0:T(8,128)}, u32[]{:S(2)}) copy-start(f32[16,32,128]{2,1,0:T(8,128)} %copy-done.2) | copy-start | bytes 786436
  451.8 25.1 %copy-start.5 = (f32[16,32,128]{2,1,0:T(8,128)S(1)}, f32[16,32,128]{2,1,0:T(8,128)}, u32[]{:S(2)}) copy-start(f32[16,32,128]{2,1,0:T(8,128)} %get-tuple-element.18) | copy-start | bytes 786436
  468.1 8.9 %copy-start.9 = (f32[16,32,128]{2,1,0:T(8,128)S(1)}, f32[16,32,128]{2,1,0:T(8,128)}, u32[]{:S(2)}) copy-start(f32[16,32,128]{2,1,0:T(8,128)} %copy-done.8) | copy-start | bytes 786436
  468.1 42.1 %copy-start.7 = (f32[16,32,128]{2,1,0:T(8,128)S(1)}, f32[16,32,128]{2,1,0:T(8,128)}, u32[]{:S(2)}) copy-start(f32[16,32,128]{2,1,0:T(8,128)} %param.8) | copy-start | bytes 786436
  479.3 32.0 %copy-start = (f32[16,32,128]{2,1,0:T(8,128)}, f32[16,32,128]{2,1,0:T(8,128)S(1)}, u32[]{:S(2)}) copy-start(f32[16,32,128]{2,1,0:T(8,128)S(1)} %fusion.45) | copy-start | bytes 786436
  479.3 6.2 %collective-permute-start.31 = (f32[1,32,128]{2,1,0:T(8,128)S(1)}, f32[1,32,128]{2,1,0:T(8,128)S(1)}, u32[]{:S(2)}, u32[]{:S(2)}) collective-permute-start(f32[1,32,128]{2,1,0:T(8,128)S(1)} %get-tuple-element.45), channel_id=1, source_target_pairs={{32,0},{64,32},{96,64},{128,96},{160,128},{192,160},{224,192},{256... | collective-permute-start | bytes 49160 | tf_op jit(solution)/shard_map/ppermute | solution.py:20
  482.7 7.5 %collective-permute-start.30 = (f32[1,32,128]{2,1,0:T(8,128)S(1)}, f32[1,32,128]{2,1,0:T(8,128)S(1)}, u32[]{:S(2)}, u32[]{:S(2)}) collective-permute-start(f32[1,32,128]{2,1,0:T(8,128)S(1)} %get-tuple-element.44), channel_id=1, source_target_pairs={{0,32},{32,64},{64,96},{96,128},{128,160},{160,192},{192,224},{224... | collective-permute-start | bytes 49160 | tf_op jit(solution)/shard_map/ppermute | solution.py:19
  490.2 5.3 %collective-permute-start.33 = (f32[18,1,128]{2,1,0:T(1,128)S(1)}, f32[18,1,128]{2,1,0:T(1,128)S(1)}, u32[]{:S(2)}, u32[]{:S(2)}) collective-permute-start(f32[18,1,128]{2,1,0:T(1,128)S(1)} %get-tuple-element.33), channel_id=1, source_target_pairs={{1,0},{2,1},{3,2},{4,3},{5,4},{6,5},{7,6},{9,8},{10,9},{11,10},{12... | collective-permute-start | bytes 27656 | tf_op jit(solution)/shard_map/ppermute | solution.py:20
  493.2 4.4 collective-permute-start.32
  497.9 11.1 %collective-permute-start.35 = (f32[18,34,1]{2,1,0:T(8,128)S(1)}, f32[18,34,1]{2,1,0:T(8,128)S(1)}, u32[]{:S(2)}, u32[]{:S(2)}) collective-permute-start(f32[18,34,1]{2,1,0:T(8,128)S(1)} %get-tuple-element.21), channel_id=1, source_target_pairs={{8,0},{16,8},{24,16},{9,1},{17,9},{25,17},{10,2},{18,10},{26,18},{... | collective-permute-start | bytes 7352 | tf_op jit(solution)/shard_map/ppermute | solution.py:20
  502.2 8.0 %collective-permute-start.34 = (f32[18,34,1]{2,1,0:T(8,128)S(1)}, f32[18,34,1]{2,1,0:T(8,128)S(1)}, u32[]{:S(2)}, u32[]{:S(2)}) collective-permute-start(f32[18,34,1]{2,1,0:T(8,128)S(1)} %get-tuple-element.20), channel_id=1, source_target_pairs={{0,8},{8,16},{16,24},{1,9},{9,17},{17,25},{2,10},{10,18},{18,26},{... | collective-permute-start | bytes 7352 | tf_op jit(solution)/shard_map/ppermute | solution.py:19
  (2 other events, 1.2 us)
